TPU v7x, 128 devices: a whole 4x4x4 slice. The times are simulated.
128 devices in a mesh: chan: 32 (over z, x, core), bl: 4 (over y).
Axes of the slice: x: 4, y: 4, z: 4, core: 2. Of those that a mesh axis runs over, the one named last changes fastest.
Arguments:
- visibilities: bfloat16 [1024, 1536, 2, 128], P('bl', 'chan'), may hold values from -6 to 6
- kernels: bfloat16 [64, 128, 256], replicated, may hold values from -0.1875 to 0.1875
- block_ids: int32 [4, 256, 8], P('bl'), may hold values from 0 to 255
- kernel_ids: int32 [4, 256, 8], P('bl'), may hold values from 0 to 63
- tile_counts: int32 [4, 256], P('bl'), may hold values from 1 to 8, as said below
- wedge_mask: int32 [256, 1536], P(('chan', 'bl')), may hold values 0 or 1
Outputs:
- delay_tiles: float32 [256, 2, 256, 1536], P(('chan', 'bl'))
Inputs may be any that keep to these rules, and one draw needn't show every extreme that they name: `tile_counts`: slots at or past a tile's count are ignored; in every group some tile uses all 8 slots.
All inputs are finite; a program needn't handle non-finite values. No bound on the sum of `wedge_mask` on one device may be relied on, other than what follows from the above.
Results may differ from a plain program's by a relative error of at most 0.0095.
Values may be sent and summed in bfloat16 or wider, within the bound.
A program may use at most 128 MiB of HBM per device.

v0:
```python
import math

import jax
import jax.numpy as jnp
from jax import lax
from jax.sharding import PartitionSpec as P


def delay_tables(nchan):
    chans = jnp.arange(nchan, dtype=jnp.int32)
    phase = chans[:, None] * chans[None, :] % nchan
    angle = phase.astype(jnp.float32) * (2.0 * math.pi / nchan)
    return (jnp.cos(angle).astype(jnp.bfloat16), jnp.sin(angle).astype(jnp.bfloat16))


def grid_tiles(vis_blocks, kernels, list_ids, list_kernels, list_counts):
    tiles, depth = list_ids.shape
    group_size = 16
    row_count = vis_blocks.shape[1]
    cells = kernels.shape[2]
    slots = jnp.arange(depth, dtype=jnp.int32)

    def one_group(inputs):
        group_ids, group_kernels, group_counts = inputs
        keep = (slots[None, :] < group_counts[:, None]).astype(jnp.bfloat16)
        total = jnp.zeros((group_size, row_count, cells), jnp.float32)
        for slot in range(depth):
            chosen = jnp.take(vis_blocks, group_ids[:, slot], axis=0)
            weights = (
                jnp.take(kernels, group_kernels[:, slot], axis=0) * keep[:, slot][:, None, None]
            )
            total = total + jnp.einsum(
                "trs,tsx->trx", chosen, weights, preferred_element_type=jnp.float32
            )
        return total.astype(jnp.bfloat16)

    shaped = (
        list_ids.reshape(tiles // group_size, group_size, depth),
        list_kernels.reshape(tiles // group_size, group_size, depth),
        list_counts.reshape(tiles // group_size, group_size),
    )
    return lax.map(one_group, shaped)


def local(visibilities, kernels, block_ids, kernel_ids, tile_counts, wedge_mask):
    n_chan = lax.axis_size("chan")
    n_group = lax.axis_size("bl")
    nblocks = visibilities.shape[0]
    ch_dev = visibilities.shape[1]
    block_len = kernels.shape[1]
    cells = kernels.shape[2]
    vis_blocks = visibilities.reshape(nblocks, ch_dev * 2, block_len)
    list_ids = block_ids[0]
    list_kernels = kernel_ids[0]
    list_counts = tile_counts[0]
    tiles = list_ids.shape[0]
    owned = wedge_mask.shape[0]
    order = jnp.arange(tiles, dtype=jnp.int32)
    group_of = order // (n_chan * owned)
    column = order // owned % n_chan
    inner = order % owned
    source = (column * n_group + group_of) * owned + inner
    list_ids = jnp.take(list_ids, source, axis=0)
    list_kernels = jnp.take(list_kernels, source, axis=0)
    list_counts = jnp.take(list_counts, source, axis=0)
    partial_value = grid_tiles(vis_blocks, kernels, list_ids, list_kernels, list_counts)
    partial_value = partial_value.reshape(tiles, ch_dev, 2, cells)
    summed = lax.psum_scatter(partial_value, "bl", scatter_dimension=0, tiled=True).astype(
        jnp.float32
    )
    gridded = lax.all_to_all(
        summed.astype(jnp.bfloat16), "chan", split_axis=0, concat_axis=1, tiled=True
    )
    nchan = gridded.shape[1]
    cosine, sine = delay_tables(nchan)
    real_part = gridded[:, :, 0]
    imag_part = gridded[:, :, 1]
    out_real = jnp.einsum(
        "tcx,cd->txd", real_part, cosine, preferred_element_type=jnp.float32
    ) + jnp.einsum("tcx,cd->txd", imag_part, sine, preferred_element_type=jnp.float32)
    out_imag = jnp.einsum(
        "tcx,cd->txd", imag_part, cosine, preferred_element_type=jnp.float32
    ) - jnp.einsum("tcx,cd->txd", real_part, sine, preferred_element_type=jnp.float32)
    scale = 1.0 / math.sqrt(nchan)
    keep_bins = wedge_mask.astype(jnp.float32)
    return jnp.stack([out_real, out_imag], axis=1) * scale * keep_bins[:, None, None, :]


def solution(mesh):
    return jax.shard_map(
        local,
        mesh=mesh,
        in_specs=(
            P("bl", "chan", None, None),
            P(),
            P("bl", None, None),
            P("bl", None, None),
            P("bl", None),
            P(("chan", "bl"), None),
        ),
        out_specs=P(("chan", "bl"), None, None, None),
        check_vma=False,
    )
```

profile of v0, /device:TPU:1, one launch (start us, length us, event | category | flops | bytes accessed | tf_op | source)
XLA Modules:
  0.0 1790.4 jit_solution(18127652312757022134)
XLA Ops:
  13.9 1433.9 %while.11 = (s32[]{:T(128)}, bf16[16,16,96,256]{3,1,0,2:T(8,128)(2,1)}, s32[16,16,8]{1,2,0:T(8,128)}, bf16[256,96,128]{2,1,0:T(8,128)(2,1)}, s32[16,16,8]{1,2,0:...) while((s32[]{:T(128)}, bf16[16,16,96,256]{3,1,0,2:T(8,128)(2,1)}, ...), condition=%wide.region_1.5_spmd.clone, body=%wide.region_0.4_spmd.clone.sunk | while | flops 818431744 | bytes 59056412 | solution.py:42
  78.5 3.8 gather_fusion
  89.8 3.8 gather_fusion.14
  97.6 4.6 fusion.182
  168.1 3.8 gather_fusion
  179.4 3.8 gather_fusion.14
  187.2 4.6 fusion.182
  257.7 3.8 gather_fusion
  269.0 3.8 gather_fusion.14
  276.8 4.6 fusion.182
  347.3 3.8 gather_fusion
  358.5 3.8 gather_fusion.14
  366.4 4.6 fusion.182
  436.8 3.8 gather_fusion
  448.1 3.8 gather_fusion.14
  455.9 4.6 fusion.182
  526.4 3.8 gather_fusion
  537.7 3.8 gather_fusion.14
  545.5 4.6 fusion.182
  616.0 3.8 gather_fusion
  627.3 3.8 gather_fusion.14
  635.2 4.6 fusion.182
  705.6 3.8 gather_fusion
  716.9 3.8 gather_fusion.14
  724.8 4.6 fusion.182
  795.3 3.8 gather_fusion
  806.6 3.8 gather_fusion.14
  814.4 4.6 fusion.182
  884.9 3.8 gather_fusion
  896.2 3.8 gather_fusion.14
  904.0 4.6 fusion.182
  974.5 3.8 gather_fusion
  985.8 3.8 gather_fusion.14
  993.6 4.6 fusion.182
  1064.2 3.8 gather_fusion
  1083.3 4.6 fusion.182
  1172.9 4.6 fusion.182
  1262.5 4.6 fusion.182
  1352.2 4.6 fusion.182
  1441.8 4.6 fusion.182
  1447.8 117.9 %reduce-scatter.2.cloned.1.call-done = bf16[64,48,2,256]{3,0,2,1:T(8,128)(2,1)} async-done(((bf16[256,48,2,256]{3,0,2,1:T(8,128)(2,1)}), bf16[64,48,2,256]{3,0,2,1:T(8,128)(2,1)}) %reduce-scatter.2.cloned.1.call-update) | async-done | bytes 3145744 | tf_op jit(solution)/shard_map/reduce_scatter | solution.py:68
  1565.7 6.8 copy.35
  1572.5 8.3 all-to-all-start
  1580.9 38.9 %all-to-all-done = bf16[64,48,2,256]{3,2,1,0:T(2,128)(2,1)S(1)} async-done(((bf16[64,48,2,256]{3,2,1,0:T(2,128)(2,1)}), bf16[64,48,2,256]{3,2,1,0:T(2,128)(2,1)S(1)}, u32[]{:S(2)}, u32[]{:S(2)}) %all-to-all-start) | async-done | bytes 3145760 | tf_op jit(solution)/shard_map/all_to_all | solution.py:71
  1621.2 39.4 %fusion.77 = f32[2,256,1536]{2,1,0:T(8,128)S(1)} fusion(bf16[2,1536,256]{2,1,0:T(8,128)(2,1)S(1)} %slice_bitcast_fusion.27), kind=kOutput, calls=%fused_computation.169 | convolution fusion | flops 2439512064 | bytes 4718592 | tf_op jit(solution)/shard_map/tcx,cd->txd/dot_general | solution.py:80
  1660.6 39.6 %fusion.75 = f32[2,256,1536]{2,1,0:T(8,128)S(1)} fusion(bf16[2,1536,256]{2,1,0:T(8,128)(2,1)S(1)} %slice_bitcast_fusion.26), kind=kOutput, calls=%fused_computation.168 | convolution fusion | flops 2439512064 | bytes 4718592 | tf_op jit(solution)/shard_map/tcx,cd->txd/dot_general | solution.py:83
  1700.2 39.6 %fusion.92 = f32[2,1,256,1536]{3,2,0,1:T(8,128)S(1)} fusion(f32[2,256,1536]{2,1,0:T(8,128)S(1)} %fusion.77, bf16[2,1536,256]{2,1,0:T(8,128)(2,1)S(1)} %slice_bitcast_fusion.29), kind=kOutput, calls=%fused_computation.175 | convolution fusion | flops 2440298496 | bytes 7864320 | tf_op jit(solution)/shard_map/tcx,cd->txd/dot_general | solution.py:78
  1739.9 39.4 %fusion.89 = f32[2,1,256,1536]{3,2,0,1:T(8,128)S(1)} fusion(f32[2,256,1536]{2,1,0:T(8,128)S(1)} %fusion.75, bf16[2,1536,256]{2,1,0:T(8,128)(2,1)S(1)} %slice_bitcast_fusion.28), kind=kOutput, calls=%fused_computation.174 | convolution fusion | flops 2440298496 | bytes 7864320 | tf_op jit(solution)/shard_map/tcx,cd->txd/dot_general | solution.py:81
  (746 shorter events, 1284.3 us)
Async XLA Ops:
  6.5 4.7 copy-start
  6.5 1559.2 %reduce-scatter.2.cloned.1.call-start = ((), (), s32[]{:S(2)}) async-start(), calls=%async_computation.2 | async-start | bytes 15728640 | tf_op jit(solution)/shard_map/reduce_scatter | solution.py:68
  1572.5 8.3 copy-start.2
  1572.5 47.3 %all-to-all-start = ((bf16[64,48,2,256]{3,2,1,0:T(2,128)(2,1)}), bf16[64,48,2,256]{3,2,1,0:T(2,128)(2,1)S(1)}, u32[]{:S(2)}, u32[]{:S(2)}) async-start(bf16[64,48,2,256]{3,2,1,0:T(2,128)(2,1)} %copy.35), calls=%async_computation.1 | async-start | bytes 6291456 | tf_op jit(solution)/shard_map/all_to_all | solution.py:71
  1779.3 3.9 copy-start.1
Sparse Core Ops, SparseCore 0:
  1447.9 117.7 reduce-scatter.1
where the time goes:
time: 1810 us; the launch traced here: 1790 us
  local copies, waits for them, and re-layouts  975 us (54%)
  matrix products  490 us (27%)
  waiting for transfers between devices  157 us (9%)
  other arithmetic  144 us (8%)
    gather x128, local copies, waits for them, and re-layouts, one_group(): jnp.take(kernels, group_kernels[:, slot], axis=0)  467 us
    gather x128, local copies, waits for them, and re-layouts, one_group(): chosen = jnp.take(vis_blocks, group_ids[:, slot], axis=0)  436 us
    dot_general x128, matrix products, one_group(): jnp.einsum('trs,tsx->trx', chosen, weights, preferred_element_type=jnp.fl...  332 us
    gather x257, other arithmetic  122 us
    reduce_scatter x1, waiting for transfers between devices, local(): lax.psum_scatter(partial_value, 'bl', scatter_dimension=0, tiled=True)  118 us
    dot_general x1, matrix products, local(): jnp.einsum('tcx,cd->txd', real_part, cosine, preferred_element_type=jnp.f...  39.6 us
    dot_general x1, matrix products, local(): jnp.einsum('tcx,cd->txd', real_part, sine, preferred_element_type=jnp.flo...  39.6 us
    dot_general x1, matrix products, local(): jnp.einsum('tcx,cd->txd', imag_part, cosine, preferred_element_type=jnp.f...  39.4 us
  transfers between devices with their start and end apart: 2, of which 2 were waited for; matrix products, arithmetic and copies ran while one was open for 0% of the time, Pallas kernels for 0%

commit v1 on v0

v1 whole, which is shorter than its diff:
```python
import functools
import math

import jax
import jax.numpy as jnp
import ml_dtypes
import numpy as np
from jax import lax
from jax.experimental import pallas as pl
from jax.experimental.pallas import tpu as pltpu
from jax.sharding import PartitionSpec as P

MESH = pl.DeviceIdType.MESH
STAGES = 16
PER = 4


def tables(nchan):
    chans = np.arange(nchan, dtype=np.int64)
    phase = chans[:, None] * chans[None, :] % nchan
    angle = phase.astype(np.float32) * np.float32(2.0 * math.pi / nchan)
    cosine, sine = np.cos(angle), np.sin(angle)
    real = np.stack([cosine, sine], axis=1).reshape(2 * nchan, nchan)
    imag = np.stack([-sine, cosine], axis=1).reshape(2 * nchan, nchan)
    return real.astype(ml_dtypes.bfloat16), imag.astype(ml_dtypes.bfloat16)


def grid_kernel(
    n_chan, n_bl, bid, kid, cnt, vis_hbm, ker_hbm, grid_out,
    vis, ker, opp, to_right, to_left, opp_in_a, opp_in_b, from_left, from_right, own,
    load_sem, opp_s, opp_r, nbr_s, nbr_r, own_s, own_r,
):
    chan = lax.axis_index("chan")
    y = lax.axis_index("bl")
    right, left = lax.rem(y + 1, n_bl), lax.rem(y + n_bl - 1, n_bl)
    far = lax.rem(y + 2, n_bl)
    blocks = vis.shape[0]
    kinds = ker_hbm.shape[0]
    cut = blocks // 4
    loads = [
        pltpu.make_async_copy(
            vis_hbm.at[pl.ds(q * cut, cut)], vis.at[pl.ds(q * cut, cut)], load_sem.at[q]
        )
        for q in range(4)
    ] + [
        pltpu.make_async_copy(
            ker_hbm.at[pl.ds(q * 32, 32)], ker.at[pl.ds(q * 32, 32)], load_sem.at[4 + q]
        )
        for q in range(2)
    ]
    for one in loads:
        one.start()
    ker[kinds] = jnp.zeros(ker.shape[1:], ker.dtype)

    barrier = pltpu.get_barrier_semaphore()

    def greet(o, carry):
        pl.semaphore_signal(
            barrier, inc=1, device_id=(lax.rem(chan + o, n_chan), y), device_id_type=MESH
        )
        return carry

    lax.fori_loop(1, n_chan, greet, 0)
    for other in (left, right):
        pl.semaphore_signal(barrier, inc=1, device_id=(chan, other), device_id_type=MESH)
    pl.semaphore_wait(barrier, n_chan + 1)
    for one in loads:
        one.wait()

    core = lax.rem(chan, 2)
    col = lax.rem(lax.div(chan, 2), 4)
    row = lax.div(chan, 8)

    def owner(s, e):
        m = STAGES - 1 - s
        dz = lax.rem(m, 4)
        dx = lax.rem(lax.div(m, 4) + m, 4)
        return (lax.rem(row + dz, 4) * 4 + lax.rem(col + dx, 4)) * 2 + lax.rem(core + e, 2)

    def partial(tile):
        count = cnt[0, tile]
        left_side, right_side = [], []
        for k in range(8):
            b = bid[tile, k]
            q = jnp.where(k < count, kid[tile, k], kinds)
            left_side.append(vis[b])
            right_side.append(ker[q])
        return jnp.dot(
            jnp.concatenate(left_side, axis=1),
            jnp.concatenate(right_side, axis=0),
            preferred_element_type=jnp.float32,
        )

    def tile_of(s, j, plane):
        return (owner(s, lax.div(j, 2)) * n_bl + plane) * 2 + lax.rem(j, 2)

    def remote(src, dst, send, recv, plane):
        return pltpu.make_async_remote_copy(
            src_ref=src, dst_ref=dst, send_sem=send, recv_sem=recv,
            device_id=(chan, plane), device_id_type=MESH,
        )

    def opp_copies(s):
        return (
            remote(opp.at[s, pl.ds(0, 2)], opp_in_a.at[s], opp_s.at[0, s], opp_r.at[0, s], left),
            remote(opp.at[s, pl.ds(2, 2)], opp_in_b.at[s], opp_s.at[1, s], opp_r.at[1, s], right),
        )

    def nbr_copies(s):
        return (
            remote(to_left.at[s], from_right.at[s], nbr_s.at[0, s], nbr_r.at[0, s], left),
            remote(to_right.at[s], from_left.at[s], nbr_s.at[1, s], nbr_r.at[1, s], right),
        )

    def own_copy(s, e):
        return pltpu.make_async_remote_copy(
            src_ref=own.at[s, pl.ds(2 * e, 2)],
            dst_ref=grid_out.at[:, chan],
            send_sem=own_s.at[s, e], recv_sem=own_r.at[s, e],
            device_id=(owner(s, e), y), device_id_type=MESH,
        )

    def self_copy():
        return pltpu.make_async_copy(
            own.at[STAGES - 1, pl.ds(0, 2)], grid_out.at[:, chan], own_r.at[STAGES - 1, 0]
        )

    def step(it, carry):
        @pl.when(it < STAGES)
        def _():
            s = it

            def one(j, c):
                opp[s, j] = partial(tile_of(s, j, far)).astype(jnp.bfloat16)
                return c

            lax.fori_loop(0, PER, one, 0)
            for copy in opp_copies(s):
                copy.start()

        @pl.when((it >= 1) & (it < STAGES + 1))
        def _():
            s = it - 1
            for copy in opp_copies(s):
                copy.wait_recv()
            go_left, go_right = nbr_copies(s)

            def plain(j, c):
                to_right[s, j] = partial(tile_of(s, j, right)).astype(jnp.bfloat16)
                to_left[s, j + 2] = partial(tile_of(s, j + 2, left)).astype(jnp.bfloat16)
                return c

            def added(j, c):
                to_right[s, j + 2] = (
                    partial(tile_of(s, j + 2, right)) + opp_in_b[s, j].astype(jnp.float32)
                ).astype(jnp.bfloat16)
                to_left[s, j] = (
                    partial(tile_of(s, j, left)) + opp_in_a[s, j].astype(jnp.float32)
                ).astype(jnp.bfloat16)
                return c

            lax.fori_loop(0, 2, plain, 0)
            lax.fori_loop(0, 2, added, 0)
            go_left.start()
            go_right.start()

        @pl.when(it >= 2)
        def _():
            s = it - 2
            for copy in nbr_copies(s):
                copy.wait_recv()

            def one(j, c):
                total = partial(tile_of(s, j, y))
                total += from_left[s, j].astype(jnp.float32)
                total += from_right[s, j].astype(jnp.float32)
                own[s, j] = total.astype(jnp.bfloat16)
                return c

            lax.fori_loop(0, PER, one, 0)

            @pl.when(s < STAGES - 1)
            def _():
                own_copy(s, 0).start()

            own_copy(s, 1).start()

            @pl.when(s == STAGES - 1)
            def _():
                self_copy().start()

        return carry

    lax.fori_loop(0, STAGES + 2, step, 0)

    def drain(s, carry):
        for copy in opp_copies(s):
            copy.wait_send()
        for copy in nbr_copies(s):
            copy.wait_send()

        @pl.when(s < STAGES - 1)
        def _():
            own_copy(s, 0).wait()

        own_copy(s, 1).wait()
        return carry

    lax.fori_loop(0, STAGES, drain, 0)
    self_copy().wait()


def local(n_chan, n_bl, real_table, imag_table, visibilities, kernels, block_ids, kernel_ids, tile_counts, wedge_mask):
    blocks, ch_dev = visibilities.shape[:2]
    length, cells = kernels.shape[1:]
    rows = ch_dev * 2
    bf16 = jnp.bfloat16
    stage = (STAGES, PER, rows, cells)
    half = (STAGES, PER // 2, rows, cells)
    any_space = pl.BlockSpec(memory_space=pl.ANY)
    smem = pl.BlockSpec(memory_space=pltpu.SMEM)
    grids = pl.pallas_call(
        functools.partial(grid_kernel, n_chan, n_bl),
        out_shape=jax.ShapeDtypeStruct((2, n_chan, rows, cells), bf16),
        in_specs=[smem, smem, smem, any_space, any_space],
        out_specs=any_space,
        scratch_shapes=[
            pltpu.VMEM((blocks, rows, length), bf16),
            pltpu.VMEM((kernels.shape[0] + 1, length, cells), bf16),
            pltpu.VMEM(stage, bf16),
            pltpu.VMEM(stage, bf16),
            pltpu.VMEM(stage, bf16),
            pltpu.VMEM(half, bf16),
            pltpu.VMEM(half, bf16),
            pltpu.VMEM(stage, bf16),
            pltpu.VMEM(stage, bf16),
            pltpu.VMEM(stage, bf16),
            pltpu.SemaphoreType.DMA((6,)),
            pltpu.SemaphoreType.DMA((2, STAGES)),
            pltpu.SemaphoreType.DMA((2, STAGES)),
            pltpu.SemaphoreType.DMA((2, STAGES)),
            pltpu.SemaphoreType.DMA((2, STAGES)),
            pltpu.SemaphoreType.DMA((STAGES, 2)),
            pltpu.SemaphoreType.DMA((STAGES, 2)),
        ],
        compiler_params=pltpu.CompilerParams(
            collective_id=0, has_side_effects=True, vmem_limit_bytes=44 << 20
        ),
        name="grid_exchange",
    )(
        block_ids[0], kernel_ids[0], tile_counts,
        visibilities.reshape(blocks, rows, length), kernels,
    )
    nchan = n_chan * ch_dev
    gridded = grids.reshape(2, 2 * nchan, cells)
    keep = wedge_mask.astype(jnp.float32)[:, None, None, :]
    scale = 1.0 / math.sqrt(nchan)
    out_real = jnp.einsum("tkx,kd->txd", gridded, real_table, preferred_element_type=jnp.float32)
    out_imag = jnp.einsum("tkx,kd->txd", gridded, imag_table, preferred_element_type=jnp.float32)
    return jnp.stack([out_real, out_imag], axis=1) * scale * keep


def solution(mesh):
    def run(visibilities, *rest):
        real_table, imag_table = tables(visibilities.shape[1])
        return jax.shard_map(
            functools.partial(
                local, mesh.shape["chan"], mesh.shape["bl"],
                jnp.asarray(real_table), jnp.asarray(imag_table),
            ),
            mesh=mesh,
            in_specs=(
                P("bl", "chan", None, None),
                P(),
                P("bl", None, None),
                P("bl", None, None),
                P("bl", None),
                P(("chan", "bl"), None),
            ),
            out_specs=P(("chan", "bl"), None, None, None),
            check_vma=False,
        )(visibilities, *rest)

    return run
```

time: 1810 us -> 144 us (0.08); the launches traced: 1790 us -> 144 us
  local copies, waits for them, and re-layouts: 975 us -> 7.66 us
  matrix products: 490 us -> 10.4 us
  waiting for transfers between devices: 157 us -> 0 us
  other arithmetic: 144 us -> 1.44 us
  Pallas kernels: 0 us -> 124 us
    gather x260 -> x0, local copies, waits for them, and re-layouts: 907 us -> none  [the longest x128 467 us: one_group(): jnp.take(kernels, group_kernels[:, slot], axis=0)]
    dot_general x132 -> x2, matrix products: 490 us -> 10.4 us  [the longest x1 5.29 us: local(): jnp.einsum('tkx,kd->txd', gridded, imag_table, preferred_element_type=jnp...]
    pallas_call x0 -> x1, Pallas kernels: none -> 124 us  [local(): pl.pallas_call(functools.partial(grid_kernel, n_chan, n_bl), out_shape=ja...]
    gather x258 -> x0, other arithmetic: 122 us -> none
    reduce_scatter x1 -> x0, waiting for transfers between devices: 118 us -> none  [local(): lax.psum_scatter(partial_value, 'bl', scatter_dimension=0, tiled=True)]
    all_to_all x1 -> x0, waiting for transfers between devices: 38.9 us -> none  [local(): lax.all_to_all(summed.astype(jnp.bfloat16), 'chan', split_axis=0, concat_...]
    dynamic_update_slice x16 -> x0, local copies, waits for them, and re-layouts: 22.1 us -> none  [grid_tiles(): return lax.map(one_group, shaped)]
    and x33 -> x0, other arithmetic: 20.5 us -> none  [the longest x16 10.2 us: one_group(): chosen = jnp.take(vis_blocks, group_ids[:, slot], axis=0)]
  transfers between devices with their start and end apart: 2 -> 0, of which waited for: 2 -> 0; matrix products, arithmetic and copies ran while one was open for 0% -> 0% of each run, Pallas kernels for 0% -> 0%
where the time goes in v1:
time: 144 us
  Pallas kernels  124 us (86%)
  matrix products  10.4 us (7%)
  local copies, waits for them, and re-layouts  7.66 us (5%)
  other arithmetic  1.44 us (1%)
    pallas_call x1, Pallas kernels, local(): pl.pallas_call(functools.partial(grid_kernel, n_chan, n_bl), out_shape=ja...  124 us
    dot_general x1, matrix products, local(): jnp.einsum('tkx,kd->txd', gridded, imag_table, preferred_element_type=jnp...  5.29 us
    dot_general x1, matrix products, local(): jnp.einsum('tkx,kd->txd', gridded, real_table, preferred_element_type=jnp...  5.13 us
    unnamed x10, local copies, waits for them, and re-layouts  4.51 us
    mul x1, local copies, waits for them, and re-layouts, local(): return jnp.stack([out_real, out_imag], axis=1) * scale * keep  3.15 us

profile of v1, /device:TPU:1, one launch (start us, length us, event | category | flops | bytes accessed | tf_op | source)
XLA Modules:
  0.0 144.1 jit_solution(3568753918541244333)
XLA Ops:
  0.0 0.7 convert_multiply_fusion
  0.7 0.8 copy.9
  1.5 0.8 copy.10
  2.4 0.0 copy-start
  2.4 2.2 %copy-done = bf16[64,128,256]{2,1,0:T(8,128)(2,1)S(1)} copy-done((bf16[64,128,256]{2,1,0:T(8,128)(2,1)S(1)}, bf16[64,128,256]{2,1,0:T(8,128)(2,1)}, u32[]{:S(2)}) %copy-start) | copy-done | bytes 4194328
  4.6 0.0 copy-start.1
  4.6 0.7 copy-done.1
  5.2 0.0 copy-start.2
  5.2 124.5 %grid_exchange.1 = bf16[2,32,96,256]{3,2,1,0:T(8,128)(2,1)S(1)} custom-call(s32[256,8]{1,0:T(8,128)S(1)} %bitcast.16, s32[256,8]{1,0:T(8,128)S(1)} %bitcast.17, s32[1,256]{1,0:T(1,128)S(1)} %copy-done.1, bf16[256,96,128]{2,1,0:T(8,128)(2,1)} %bitcast.18, bf16[64,128,256]{2,1,0:T(8,128)(2,1)S(1)} %copy-done), custom_call_target="tpu_custom_call" | custom-call | tf_op jit(solution)/shard_map/grid_exchange/pallas_call | solution.py:222
  129.7 0.0 copy-done.2
  129.7 0.0 copy-start.3
  129.7 5.3 %convolution_bitcast_fusion = f32[2,1,256,1536]{3,2,0,1:T(8,128)S(1)} fusion(bf16[2,3072,256]{2,1,0:T(8,128)(2,1)S(1)} %bitcast.14, bf16[3072,1536,1]{1,0,2:T(8,128)(2,1)S(1)} %copy-done.2), kind=kOutput, calls=%fused_computation.1 | convolution fusion | flops 4831838208 | bytes 15728640 | tf_op jit(solution)/shard_map/tkx,kd->txd/dot_general | solution.py:259
  135.0 0.0 copy-done.3
  135.0 5.1 %convolution_bitcast_fusion.1 = f32[2,1,256,1536]{3,2,0,1:T(8,128)S(1)} fusion(bf16[2,3072,256]{2,1,0:T(8,128)(2,1)S(1)} %bitcast.15, bf16[3072,1536,1]{1,0,2:T(8,128)(2,1)S(1)} %copy-done.3), kind=kOutput, calls=%fused_computation.2 | convolution fusion | flops 4831838208 | bytes 15728640 | tf_op jit(solution)/shard_map/tkx,kd->txd/dot_general | solution.py:258
  140.2 0.7 maximum_multiply_fusion
  140.9 3.1 %copy.13 = f32[2,2,256,1536]{3,2,1,0:T(8,128)} copy(f32[2,2,256,1536]{3,2,0,1:T(8,128)S(1)} %maximum_multiply_fusion) | data formatting | bytes 12582912 | tf_op jit(solution)/shard_map/mul | solution.py:260
Async XLA Ops:
  2.4 2.2 %copy-start = (bf16[64,128,256]{2,1,0:T(8,128)(2,1)S(1)}, bf16[64,128,256]{2,1,0:T(8,128)(2,1)}, u32[]{:S(2)}) copy-start(bf16[64,128,256]{2,1,0:T(8,128)(2,1)} %ker_hbm.1) | copy-start | bytes 12582916
  4.6 0.7 copy-start.1
  5.2 124.5 %copy-start.2 = (bf16[3072,1536,1]{1,0,2:T(8,128)(2,1)S(1)}, bf16[3072,1536,1]{1,0,2:T(8,128)(2,1)}, u32[]{:S(2)}) copy-start(bf16[3072,1536,1]{1,0,2:T(8,128)(2,1)} %constant.14) | copy-start | bytes 28311556
  129.7 5.3 %copy-start.3 = (bf16[3072,1536,1]{1,0,2:T(8,128)(2,1)S(1)}, bf16[3072,1536,1]{1,0,2:T(8,128)(2,1)}, u32[]{:S(2)}) copy-start(bf16[3072,1536,1]{1,0,2:T(8,128)(2,1)} %constant.13) | copy-start | bytes 28311556

commit v2 on v1

--- a/solution.py
+++ b/solution.py
@@ -15,19 +15,25 @@
 PER = 4
 
 
-def tables(nchan):
-    chans = np.arange(nchan, dtype=np.int64)
-    phase = chans[:, None] * chans[None, :] % nchan
-    angle = phase.astype(np.float32) * np.float32(2.0 * math.pi / nchan)
-    cosine, sine = np.cos(angle), np.sin(angle)
-    real = np.stack([cosine, sine], axis=1).reshape(2 * nchan, nchan)
-    imag = np.stack([-sine, cosine], axis=1).reshape(2 * nchan, nchan)
-    return real.astype(ml_dtypes.bfloat16), imag.astype(ml_dtypes.bfloat16)
+def tables(nchan, ch_dev):
+    half = nchan // 2
+    delays = np.arange(half, dtype=np.int64)
+    result = []
+    for odd in range(2):
+        chans = np.arange(nchan, dtype=np.int64).reshape(nchan // ch_dev, ch_dev)[:, odd::2]
+        phase = chans[:, :, None] * delays % nchan
+        angle = phase.astype(np.float32) * np.float32(2.0 * math.pi / nchan)
+        cosine, sine = np.cos(angle), np.sin(angle)
+        real = np.stack([cosine, sine], axis=1)
+        imag = np.stack([-sine, cosine], axis=1)
+        both = np.concatenate([real, imag], axis=3).reshape(nchan, nchan)
+        result.append(both.astype(ml_dtypes.bfloat16))
+    return np.stack(result)
 
 
 def grid_kernel(
-    n_chan, n_bl, bid, kid, cnt, vis_hbm, ker_hbm, grid_out,
-    vis, ker, opp, to_right, to_left, opp_in_a, opp_in_b, from_left, from_right, own,
+    n_chan, n_bl, bid_hbm, kid_hbm, cnt_hbm, vis_hbm, ker_hbm, grid_out,
+    bid, kid, cnt, vis, ker, sums, opp, to_right, to_left, opp_in_a, opp_in_b, from_left, from_right, own,
     load_sem, opp_s, opp_r, nbr_s, nbr_r, own_s, own_r,
 ):
     chan = lax.axis_index("chan")
@@ -37,6 +43,7 @@
     blocks = vis.shape[0]
     kinds = ker_hbm.shape[0]
     cut = blocks // 4
+    rows = vis.shape[1]
     loads = [
         pltpu.make_async_copy(
             vis_hbm.at[pl.ds(q * cut, cut)], vis.at[pl.ds(q * cut, cut)], load_sem.at[q]
@@ -47,6 +54,9 @@
             ker_hbm.at[pl.ds(q * 32, 32)], ker.at[pl.ds(q * 32, 32)], load_sem.at[4 + q]
         )
         for q in range(2)
+    ] + [
+        pltpu.make_async_copy(src, dst, load_sem.at[6 + q])
+        for q, (src, dst) in enumerate(((bid_hbm, bid), (kid_hbm, kid), (cnt_hbm, cnt)))
     ]
     for one in loads:
         one.start()
@@ -81,8 +91,8 @@
         count = cnt[0, tile]
         left_side, right_side = [], []
         for k in range(8):
-            b = bid[tile, k]
-            q = jnp.where(k < count, kid[tile, k], kinds)
+            b = bid[k, tile]
+            q = jnp.where(k < count, kid[k, tile], kinds)
             left_side.append(vis[b])
             right_side.append(ker[q])
         return jnp.dot(
@@ -92,7 +102,7 @@
         )
 
     def tile_of(s, j, plane):
-        return (owner(s, lax.div(j, 2)) * n_bl + plane) * 2 + lax.rem(j, 2)
+        return (owner(s, j // 2) * n_bl + plane) * 2 + j % 2
 
     def remote(src, dst, send, recv, plane):
         return pltpu.make_async_remote_copy(
@@ -115,14 +125,14 @@
     def own_copy(s, e):
         return pltpu.make_async_remote_copy(
             src_ref=own.at[s, pl.ds(2 * e, 2)],
-            dst_ref=grid_out.at[:, chan],
+            dst_ref=grid_out.at[:, :, chan],
             send_sem=own_s.at[s, e], recv_sem=own_r.at[s, e],
             device_id=(owner(s, e), y), device_id_type=MESH,
         )
 
     def self_copy():
         return pltpu.make_async_copy(
-            own.at[STAGES - 1, pl.ds(0, 2)], grid_out.at[:, chan], own_r.at[STAGES - 1, 0]
+            own.at[STAGES - 1, pl.ds(0, 2)], grid_out.at[:, :, chan], own_r.at[STAGES - 1, 0]
         )
 
     def step(it, carry):
@@ -130,11 +140,8 @@
         def _():
             s = it
 
-            def one(j, c):
+            for j in range(PER):
                 opp[s, j] = partial(tile_of(s, j, far)).astype(jnp.bfloat16)
-                return c
-
-            lax.fori_loop(0, PER, one, 0)
             for copy in opp_copies(s):
                 copy.start()
 
@@ -145,22 +152,16 @@
                 copy.wait_recv()
             go_left, go_right = nbr_copies(s)
 
-            def plain(j, c):
+            for j in range(2):
                 to_right[s, j] = partial(tile_of(s, j, right)).astype(jnp.bfloat16)
                 to_left[s, j + 2] = partial(tile_of(s, j + 2, left)).astype(jnp.bfloat16)
-                return c
-
-            def added(j, c):
+            for j in range(2):
                 to_right[s, j + 2] = (
                     partial(tile_of(s, j + 2, right)) + opp_in_b[s, j].astype(jnp.float32)
                 ).astype(jnp.bfloat16)
                 to_left[s, j] = (
                     partial(tile_of(s, j, left)) + opp_in_a[s, j].astype(jnp.float32)
                 ).astype(jnp.bfloat16)
-                return c
-
-            lax.fori_loop(0, 2, plain, 0)
-            lax.fori_loop(0, 2, added, 0)
             go_left.start()
             go_right.start()
 
@@ -170,14 +171,21 @@
             for copy in nbr_copies(s):
                 copy.wait_recv()
 
-            def one(j, c):
+            for j in range(PER):
                 total = partial(tile_of(s, j, y))
                 total += from_left[s, j].astype(jnp.float32)
                 total += from_right[s, j].astype(jnp.float32)
-                own[s, j] = total.astype(jnp.bfloat16)
-                return c
-
-            lax.fori_loop(0, PER, one, 0)
+                for lane in range(sums.shape[1]):
+                    sums[j, lane] = total[:, lane * 128 : lane * 128 + 128]
+                for odd in range(2):
+                    sorted_rows = [
+                        jnp.concatenate(
+                            [sums[j, lane, pl.ds(2 * odd + p, rows // 4, stride=4)] for p in range(2)],
+                            axis=0,
+                        )
+                        for lane in range(sums.shape[1])
+                    ]
+                    own[s, j, odd] = jnp.concatenate(sorted_rows, axis=1).astype(jnp.bfloat16)
 
             @pl.when(s < STAGES - 1)
             def _():
@@ -210,7 +218,41 @@
     self_copy().wait()
 
 
-def local(n_chan, n_bl, real_table, imag_table, visibilities, kernels, block_ids, kernel_ids, tile_counts, wedge_mask):
+def delay_kernel(grids, table, keep, out_hbm, left, out, sem):
+    tiles, parities, nchan, cells = grids.shape
+    half = nchan // 2
+    width = cells
+    scale = 1.0 / math.sqrt(nchan)
+    copies = []
+    for t in range(tiles):
+        for odd in range(parities):
+            left[t, odd] = grids[t, odd].T
+        for part in range(2):
+            for q in range(half // width):
+                at = part * half + q * width
+                even_sum, odd_sum = (
+                    jnp.dot(
+                        left[t, odd], table[odd, :, at : at + width],
+                        preferred_element_type=jnp.float32,
+                    )
+                    for odd in range(2)
+                )
+                for side, value in enumerate((even_sum + odd_sum, even_sum - odd_sum)):
+                    lane = side * half + q * width
+                    bins = keep[t : t + 1, lane : lane + width].astype(jnp.float32) * scale
+                    out[t, part, :, lane : lane + width] = value * bins
+                    copy = pltpu.make_async_copy(
+                        out.at[t, part, :, pl.ds(lane, width)],
+                        out_hbm.at[t, part, :, pl.ds(lane, width)],
+                        sem.at[len(copies)],
+                    )
+                    copy.start()
+                    copies.append(copy)
+    for copy in copies:
+        copy.wait()
+
+
+def local(n_chan, n_bl, table, visibilities, kernels, block_ids, kernel_ids, tile_counts, wedge_mask):
     blocks, ch_dev = visibilities.shape[:2]
     length, cells = kernels.shape[1:]
     rows = ch_dev * 2
@@ -218,15 +260,19 @@
     stage = (STAGES, PER, rows, cells)
     half = (STAGES, PER // 2, rows, cells)
     any_space = pl.BlockSpec(memory_space=pl.ANY)
-    smem = pl.BlockSpec(memory_space=pltpu.SMEM)
+    hbm = pl.BlockSpec(memory_space=pltpu.HBM)
     grids = pl.pallas_call(
         functools.partial(grid_kernel, n_chan, n_bl),
-        out_shape=jax.ShapeDtypeStruct((2, n_chan, rows, cells), bf16),
-        in_specs=[smem, smem, smem, any_space, any_space],
+        out_shape=jax.ShapeDtypeStruct((2, 2, n_chan, rows // 2, cells), bf16),
+        in_specs=[hbm] * 5,
         out_specs=any_space,
         scratch_shapes=[
+            pltpu.SMEM(block_ids.shape[:0:-1], jnp.int32),
+            pltpu.SMEM(block_ids.shape[:0:-1], jnp.int32),
+            pltpu.SMEM(tile_counts.shape, jnp.int32),
             pltpu.VMEM((blocks, rows, length), bf16),
             pltpu.VMEM((kernels.shape[0] + 1, length, cells), bf16),
+            pltpu.VMEM((PER, cells // 128, rows, 128), jnp.float32),
             pltpu.VMEM(stage, bf16),
             pltpu.VMEM(stage, bf16),
             pltpu.VMEM(stage, bf16),
@@ -234,8 +280,8 @@
             pltpu.VMEM(half, bf16),
             pltpu.VMEM(stage, bf16),
             pltpu.VMEM(stage, bf16),
-            pltpu.VMEM(stage, bf16),
-            pltpu.SemaphoreType.DMA((6,)),
+            pltpu.VMEM((STAGES, PER, 2, rows // 2, cells), bf16),
+            pltpu.SemaphoreType.DMA((9,)),
             pltpu.SemaphoreType.DMA((2, STAGES)),
             pltpu.SemaphoreType.DMA((2, STAGES)),
             pltpu.SemaphoreType.DMA((2, STAGES)),
@@ -248,25 +294,39 @@
         ),
         name="grid_exchange",
     )(
-        block_ids[0], kernel_ids[0], tile_counts,
+        block_ids[0].T, kernel_ids[0].T, tile_counts,
         visibilities.reshape(blocks, rows, length), kernels,
     )
     nchan = n_chan * ch_dev
-    gridded = grids.reshape(2, 2 * nchan, cells)
-    keep = wedge_mask.astype(jnp.float32)[:, None, None, :]
-    scale = 1.0 / math.sqrt(nchan)
-    out_real = jnp.einsum("tkx,kd->txd", gridded, real_table, preferred_element_type=jnp.float32)
-    out_imag = jnp.einsum("tkx,kd->txd", gridded, imag_table, preferred_element_type=jnp.float32)
-    return jnp.stack([out_real, out_imag], axis=1) * scale * keep
+    tiles = wedge_mask.shape[0]
+    vmem = pl.BlockSpec(memory_space=pltpu.VMEM)
+    result = (tiles, 2, cells, nchan)
+    return pl.pallas_call(
+        delay_kernel,
+        out_shape=jax.ShapeDtypeStruct(result, jnp.float32),
+        in_specs=[vmem, vmem, vmem],
+        out_specs=hbm,
+        scratch_shapes=[
+            pltpu.VMEM((tiles, 2, cells, nchan), bf16),
+            pltpu.VMEM(result, jnp.float32),
+            pltpu.SemaphoreType.DMA((4 * tiles * nchan // 2 // cells,)),
+        ],
+        compiler_params=pltpu.CompilerParams(vmem_limit_bytes=34 << 20),
+        cost_estimate=pl.CostEstimate(
+            flops=tiles * 4 * cells * nchan * nchan, bytes_accessed=25 << 20, transcendentals=0
+        ),
+        name="delay_transform",
+    )(grids.reshape(2, 2, nchan, cells), table, wedge_mask)
 
 
 def solution(mesh):
     def run(visibilities, *rest):
-        real_table, imag_table = tables(visibilities.shape[1])
+        nchan = visibilities.shape[1]
+        table = tables(nchan, nchan // mesh.shape["chan"])
         return jax.shard_map(
             functools.partial(
                 local, mesh.shape["chan"], mesh.shape["bl"],
-                jnp.asarray(real_table), jnp.asarray(imag_table),
+                jnp.asarray(table),
             ),
             mesh=mesh,
             in_specs=(

time: 144 us -> 131 us (0.910)
  matrix products: 10.4 us -> 0 us
  local copies, waits for them, and re-layouts: 7.66 us -> 4.27 us
  Pallas kernels: 124 us -> 126 us
  other arithmetic: 1.44 us -> 0 us
    dot_general x2 -> x0, matrix products: 10.4 us -> none  [the longest x1 5.29 us: local(): jnp.einsum('tkx,kd->txd', gridded, imag_table, preferred_element_type=jnp...]
    pallas_call x0 -> x1, Pallas kernels: none -> 6.85 us  [local(): pl.pallas_call(delay_kernel, out_shape=jax.ShapeDtypeStruct(result, jnp.f...]
    pallas_call x1, Pallas kernels: 124 us -> 119 us  [local(): pl.pallas_call(functools.partial(grid_kernel, n_chan, n_bl), out_shape=ja...]
    mul x1 -> x0, local copies, waits for them, and re-layouts: 3.15 us -> none  [local(): return jnp.stack([out_real, out_imag], axis=1) * scale * keep]
    mul x2 -> x0, other arithmetic: 1.44 us -> none  [local(): return jnp.stack([out_real, out_imag], axis=1) * scale * keep]
    unnamed x10 -> x12, local copies, waits for them, and re-layouts: 4.51 us -> 4.27 us
where the time goes in v2:
time: 131 us; the launch traced here: 130 us
  Pallas kernels  126 us (96%)
  local copies, waits for them, and re-layouts  4.27 us (3%)
    pallas_call x1, Pallas kernels, local(): pl.pallas_call(functools.partial(grid_kernel, n_chan, n_bl), out_shape=ja...  119 us
    pallas_call x1, Pallas kernels, local(): pl.pallas_call(delay_kernel, out_shape=jax.ShapeDtypeStruct(result, jnp.f...  6.85 us
    unnamed x12, local copies, waits for them, and re-layouts  4.27 us

profile of v2, /device:TPU:1, one launch (start us, length us, event | category | flops | bytes accessed | tf_op | source)
XLA Modules:
  0.0 130.4 jit_solution(1945562900586841852)
XLA Ops:
  0.0 0.0 copy-start.1
  0.0 2.2 %copy-done.1 = bf16[64,128,256]{2,1,0:T(8,128)(2,1)S(1)} copy-done((bf16[64,128,256]{2,1,0:T(8,128)(2,1)S(1)}, bf16[64,128,256]{2,1,0:T(8,128)(2,1)}, u32[]{:S(2)}) %copy-start.1) | copy-done | bytes 4194328
  2.2 0.0 copy-start.3
  2.2 0.7 copy-done.3
  2.9 0.0 copy-start.4
  2.9 0.7 copy-done.4
  3.6 0.0 copy-start.5
  3.6 0.7 copy-done.5
  4.3 0.0 copy-start
  4.3 0.0 copy-start.2
  4.3 119.2 %grid_exchange.1 = bf16[2,2,32,48,256]{4,3,2,1,0:T(8,128)(2,1)S(1)} custom-call(s32[8,256]{1,0:T(8,128)S(1)} %bitcast.9, s32[8,256]{1,0:T(8,128)S(1)} %bitcast.10, s32[1,256]{1,0:T(1,128)S(1)} %copy-done.5, bf16[256,96,128]{2,1,0:T(8,128)(2,1)} %bitcast.11, bf16[64,128,256]{2,1,0:T(8,128)(2,1)S(1)} %copy-done.1), custom_call_target="tpu_custom_call" | custom-call | tf_op jit(solution)/shard_map/grid_exchange/pallas_call | solution.py:264
  123.5 0.0 copy-done
  123.5 0.0 copy-done.2
  123.5 6.8 %delay_transform.1 = f32[2,2,256,1536]{3,2,1,0:T(8,128)} custom-call(bf16[2,2,1536,256]{3,2,1,0:T(8,128)(2,1)S(1)} %bitcast.8, bf16[2,1536,1536]{2,1,0:T(8,128)(2,1)S(1)} %copy-done, s32[2,1536]{1,0:T(2,128)S(1)} %copy-done.2), custom_call_target="tpu_custom_call" | custom-call | flops 4831838208 | bytes 26214400 | tf_op jit(solution)/shard_map/delay_transform/pallas_call | solution.py:304
Async XLA Ops:
  0.0 2.2 %copy-start.1 = (bf16[64,128,256]{2,1,0:T(8,128)(2,1)S(1)}, bf16[64,128,256]{2,1,0:T(8,128)(2,1)}, u32[]{:S(2)}) copy-start(bf16[64,128,256]{2,1,0:T(8,128)(2,1)} %ker_hbm.1) | copy-start | bytes 12582916
  2.2 0.7 copy-start.3
  2.9 0.7 copy-start.4
  3.6 0.7 copy-start.5
  4.3 119.2 %copy-start = (bf16[2,1536,1536]{2,1,0:T(8,128)(2,1)S(1)}, bf16[2,1536,1536]{2,1,0:T(8,128)(2,1)}, u32[]{:S(2)}) copy-start(bf16[2,1536,1536]{2,1,0:T(8,128)(2,1)} %constant.2.clone.table) | copy-start | bytes 28311556
  4.3 119.3 %copy-start.2 = (s32[2,1536]{1,0:T(2,128)S(1)}, s32[2,1536]{1,0:T(2,128)}, u32[]{:S(2)}) copy-start(s32[2,1536]{1,0:T(2,128)} %keep.1) | copy-start | bytes 36868

commit v3 on v2

--- a/solution.py
+++ b/solution.py
@@ -33,30 +33,41 @@
 
 def grid_kernel(
     n_chan, n_bl, bid_hbm, kid_hbm, cnt_hbm, vis_hbm, ker_hbm, grid_out,
-    bid, kid, cnt, vis, ker, sums, opp, to_right, to_left, opp_in_a, opp_in_b, from_left, from_right, own,
-    load_sem, opp_s, opp_r, nbr_s, nbr_r, own_s, own_r,
+    bid, kid, cnt, bid_in, kid_in, cnt_in, bid_out, kid_out, cnt_out,
+    vis_hub, vis_leaf, vis_in, ker, sums,
+    sum_own, sum_inner, sum_far, sum_outer,
+    to_inner, to_far, to_outer, from_inner, from_far, from_outer, own,
+    load_sem, vis_s, vis_r, nbr_s, nbr_r, own_s, own_r,
 ):
     chan = lax.axis_index("chan")
     y = lax.axis_index("bl")
-    right, left = lax.rem(y + 1, n_bl), lax.rem(y + n_bl - 1, n_bl)
+    core = lax.rem(chan, 2)
+    col = lax.rem(lax.div(chan, 2), 4)
+    row = lax.div(chan, 8)
+
+    role = lax.rem(y + n_bl - core, n_bl)
+    hub = lax.rem(lax.div(role + 1, 2) + 1, 2)
+    turn = 2 * lax.rem(role, 2)
+    outer = lax.rem(y + 1 + turn, n_bl)
+    inner = lax.rem(y + 3 + turn, n_bl)
     far = lax.rem(y + 2, n_bl)
-    blocks = vis.shape[0]
+
+    blocks, part_rows = vis_hub.shape[:2]
     kinds = ker_hbm.shape[0]
+    hub_at = pl.multiple_of(hub * part_rows, part_rows)
+    leaf_at = pl.multiple_of((1 - hub) * part_rows, part_rows)
     cut = blocks // 4
-    rows = vis.shape[1]
+
     loads = [
-        pltpu.make_async_copy(
-            vis_hbm.at[pl.ds(q * cut, cut)], vis.at[pl.ds(q * cut, cut)], load_sem.at[q]
-        )
-        for q in range(4)
-    ] + [
-        pltpu.make_async_copy(
-            ker_hbm.at[pl.ds(q * 32, 32)], ker.at[pl.ds(q * 32, 32)], load_sem.at[4 + q]
-        )
-        for q in range(2)
-    ] + [
-        pltpu.make_async_copy(src, dst, load_sem.at[6 + q])
-        for q, (src, dst) in enumerate(((bid_hbm, bid), (kid_hbm, kid), (cnt_hbm, cnt)))
+        pltpu.make_async_copy(src, dst, load_sem.at[q])
+        for q, (src, dst) in enumerate(
+            (
+                (bid_hbm, bid), (kid_hbm, kid), (cnt_hbm, cnt),
+                (ker_hbm, ker.at[pl.ds(0, kinds)]),
+                (vis_hbm.at[:, pl.ds(hub_at, part_rows)], vis_hub),
+                (vis_hbm.at[:, pl.ds(leaf_at, part_rows)], vis_leaf),
+            )
+        )
     ]
     for one in loads:
         one.start()
@@ -70,16 +81,34 @@
         )
         return carry
 
+    for other in (outer, inner):
+        pl.semaphore_signal(barrier, inc=1, device_id=(chan, other), device_id_type=MESH)
     lax.fori_loop(1, n_chan, greet, 0)
-    for other in (left, right):
-        pl.semaphore_signal(barrier, inc=1, device_id=(chan, other), device_id_type=MESH)
     pl.semaphore_wait(barrier, n_chan + 1)
+
+    def remote(src, dst, send, recv, plane):
+        return pltpu.make_async_remote_copy(
+            src_ref=src, dst_ref=dst, send_sem=send, recv_sem=recv,
+            device_id=(chan, plane), device_id_type=MESH,
+        )
+
+    vis_copies = [
+        remote(src, dst, vis_s.at[q], vis_r.at[q], outer)
+        for q, (src, dst) in enumerate(
+            [(bid_hbm, bid_in), (kid_hbm, kid_in), (cnt_hbm, cnt_in)]
+            + [
+                (
+                    vis_hbm.at[pl.ds(q * cut, cut), pl.ds(leaf_at, part_rows)],
+                    vis_in.at[pl.ds(q * cut, cut)],
+                )
+                for q in range(4)
+            ]
+        )
+    ]
+    for copy in vis_copies:
+        copy.start()
     for one in loads:
         one.wait()
-
-    core = lax.rem(chan, 2)
-    col = lax.rem(lax.div(chan, 2), 4)
-    row = lax.div(chan, 8)
 
     def owner(s, e):
         m = STAGES - 1 - s
@@ -87,13 +116,18 @@
         dx = lax.rem(lax.div(m, 4) + m, 4)
         return (lax.rem(row + dz, 4) * 4 + lax.rem(col + dx, 4)) * 2 + lax.rem(core + e, 2)
 
-    def partial(tile):
-        count = cnt[0, tile]
+    def tile_of(s, j, plane):
+        return (owner(s, j // 2) * n_bl + plane) * 2 + j % 2
+
+    def partial(tile, ids, sources):
+        block_of, kind_of, count_of = ids
+        count = count_of[0, tile]
         left_side, right_side = [], []
         for k in range(8):
-            b = bid[k, tile]
-            q = jnp.where(k < count, kid[k, tile], kinds)
-            left_side.append(vis[b])
+            b = block_of[k, tile]
+            q = jnp.where(k < count, kind_of[k, tile], kinds)
+            chosen = [one[b] for one in sources]
+            left_side.append(chosen[0] if len(chosen) == 1 else jnp.concatenate(chosen, axis=0))
             right_side.append(ker[q])
         return jnp.dot(
             jnp.concatenate(left_side, axis=1),
@@ -101,26 +135,38 @@
             preferred_element_type=jnp.float32,
         )
 
-    def tile_of(s, j, plane):
-        return (owner(s, j // 2) * n_bl + plane) * 2 + j % 2
-
-    def remote(src, dst, send, recv, plane):
-        return pltpu.make_async_remote_copy(
-            src_ref=src, dst_ref=dst, send_sem=send, recv_sem=recv,
-            device_id=(chan, plane), device_id_type=MESH,
-        )
-
-    def opp_copies(s):
-        return (
-            remote(opp.at[s, pl.ds(0, 2)], opp_in_a.at[s], opp_s.at[0, s], opp_r.at[0, s], left),
-            remote(opp.at[s, pl.ds(2, 2)], opp_in_b.at[s], opp_s.at[1, s], opp_r.at[1, s], right),
-        )
-
-    def nbr_copies(s):
-        return (
-            remote(to_left.at[s], from_right.at[s], nbr_s.at[0, s], nbr_r.at[0, s], left),
-            remote(to_right.at[s], from_left.at[s], nbr_s.at[1, s], nbr_r.at[1, s], right),
-        )
+    mine = (bid, kid, cnt)
+    others = (bid_out, kid_out, cnt_out)
+
+    def first(s, carry):
+        for j in range(PER):
+            sum_far[s, j] = partial(tile_of(s, j, far), mine, [vis_hub])
+            sum_inner[s, j] = partial(tile_of(s, j, inner), mine, [vis_hub])
+            sum_outer[s, j] = partial(tile_of(s, j, outer), mine, [vis_hub])
+            sum_own[s, j] = partial(tile_of(s, j, y), mine, [vis_hub, vis_leaf])
+        return carry
+
+    lax.fori_loop(0, STAGES, first, 0)
+
+    for copy in vis_copies:
+        copy.wait_recv()
+    arrived = [
+        pltpu.make_async_copy(src, dst, load_sem.at[q])
+        for q, (src, dst) in enumerate(((bid_in, bid_out), (kid_in, kid_out), (cnt_in, cnt_out)))
+    ]
+    for one in arrived:
+        one.start()
+    for one in arrived:
+        one.wait()
+
+    def far_copy(s):
+        return remote(to_far.at[s], from_far.at[s], nbr_s.at[0, s], nbr_r.at[0, s], inner)
+
+    def inner_copy(s):
+        return remote(to_inner.at[s], from_inner.at[s], nbr_s.at[1, s], nbr_r.at[1, s], inner)
+
+    def outer_copy(s):
+        return remote(to_outer.at[s], from_outer.at[s], nbr_s.at[2, s], nbr_r.at[2, s], outer)
 
     def own_copy(s, e):
         return pltpu.make_async_remote_copy(
@@ -139,48 +185,50 @@
         @pl.when(it < STAGES)
         def _():
             s = it
-
             for j in range(PER):
-                opp[s, j] = partial(tile_of(s, j, far)).astype(jnp.bfloat16)
-            for copy in opp_copies(s):
-                copy.start()
+                to_far[s, j] = (
+                    sum_far[s, j] + partial(tile_of(s, j, far), others, [vis_in])
+                ).astype(jnp.bfloat16)
+            far_copy(s).start()
+            for j in range(PER):
+                to_inner[s, j] = (
+                    sum_inner[s, j] + partial(tile_of(s, j, inner), others, [vis_in])
+                ).astype(jnp.bfloat16)
+            inner_copy(s).start()
 
         @pl.when((it >= 1) & (it < STAGES + 1))
         def _():
             s = it - 1
-            for copy in opp_copies(s):
-                copy.wait_recv()
-            go_left, go_right = nbr_copies(s)
-
-            for j in range(2):
-                to_right[s, j] = partial(tile_of(s, j, right)).astype(jnp.bfloat16)
-                to_left[s, j + 2] = partial(tile_of(s, j + 2, left)).astype(jnp.bfloat16)
-            for j in range(2):
-                to_right[s, j + 2] = (
-                    partial(tile_of(s, j + 2, right)) + opp_in_b[s, j].astype(jnp.float32)
+            far_copy(s).wait_recv()
+            for j in range(PER):
+                to_outer[s, j] = (
+                    sum_outer[s, j] + from_far[s, j].astype(jnp.float32)
                 ).astype(jnp.bfloat16)
-                to_left[s, j] = (
-                    partial(tile_of(s, j, left)) + opp_in_a[s, j].astype(jnp.float32)
-                ).astype(jnp.bfloat16)
-            go_left.start()
-            go_right.start()
+            outer_copy(s).start()
 
         @pl.when(it >= 2)
         def _():
             s = it - 2
-            for copy in nbr_copies(s):
-                copy.wait_recv()
-
+            inner_copy(s).wait_recv()
+            outer_copy(s).wait_recv()
             for j in range(PER):
-                total = partial(tile_of(s, j, y))
-                total += from_left[s, j].astype(jnp.float32)
-                total += from_right[s, j].astype(jnp.float32)
+                hub_rows = (
+                    sum_own[s, j, :part_rows]
+                    + partial(tile_of(s, j, y), others, [vis_in])
+                    + from_inner[s, j].astype(jnp.float32)
+                )
+                leaf_rows = sum_own[s, j, part_rows:] + from_outer[s, j].astype(jnp.float32)
                 for lane in range(sums.shape[1]):
-                    sums[j, lane] = total[:, lane * 128 : lane * 128 + 128]
+                    at = slice(lane * 128, lane * 128 + 128)
+                    sums[j, lane, pl.ds(hub_at, part_rows)] = hub_rows[:, at]
+                    sums[j, lane, pl.ds(leaf_at, part_rows)] = leaf_rows[:, at]
                 for odd in range(2):
                     sorted_rows = [
                         jnp.concatenate(
-                            [sums[j, lane, pl.ds(2 * odd + p, rows // 4, stride=4)] for p in range(2)],
+                            [
+                                sums[j, lane, pl.ds(2 * odd + p, part_rows // 2, stride=4)]
+                                for p in range(2)
+                            ],
                             axis=0,
                         )
                         for lane in range(sums.shape[1])
@@ -201,10 +249,11 @@
 
     lax.fori_loop(0, STAGES + 2, step, 0)
 
+    for copy in vis_copies:
+        copy.wait_send()
+
     def drain(s, carry):
-        for copy in opp_copies(s):
-            copy.wait_send()
-        for copy in nbr_copies(s):
+        for copy in (far_copy(s), inner_copy(s), outer_copy(s)):
             copy.wait_send()
 
         @pl.when(s < STAGES - 1)
@@ -257,46 +306,59 @@
     length, cells = kernels.shape[1:]
     rows = ch_dev * 2
     bf16 = jnp.bfloat16
-    stage = (STAGES, PER, rows, cells)
-    half = (STAGES, PER // 2, rows, cells)
-    any_space = pl.BlockSpec(memory_space=pl.ANY)
+    part_rows = rows // 2
+    stage = (STAGES, PER, part_rows, cells)
+    f32 = jnp.float32
     hbm = pl.BlockSpec(memory_space=pltpu.HBM)
+    ids = (block_ids.shape[2], block_ids.shape[1])
+    operands = (
+        block_ids[0].T, kernel_ids[0].T, tile_counts,
+        visibilities.reshape(blocks, rows, length), kernels,
+    )
     grids = pl.pallas_call(
         functools.partial(grid_kernel, n_chan, n_bl),
-        out_shape=jax.ShapeDtypeStruct((2, 2, n_chan, rows // 2, cells), bf16),
-        in_specs=[hbm] * 5,
-        out_specs=any_space,
+        out_shape=jax.ShapeDtypeStruct((2, 2, n_chan, part_rows, cells), bf16),
+        in_specs=[hbm] * len(operands),
+        out_specs=pl.BlockSpec(memory_space=pl.ANY),
         scratch_shapes=[
-            pltpu.SMEM(block_ids.shape[:0:-1], jnp.int32),
-            pltpu.SMEM(block_ids.shape[:0:-1], jnp.int32),
+            pltpu.SMEM(ids, jnp.int32),
+            pltpu.SMEM(ids, jnp.int32),
             pltpu.SMEM(tile_counts.shape, jnp.int32),
-            pltpu.VMEM((blocks, rows, length), bf16),
+            pltpu.VMEM(ids, jnp.int32),
+            pltpu.VMEM(ids, jnp.int32),
+            pltpu.VMEM(tile_counts.shape, jnp.int32),
+            pltpu.SMEM(ids, jnp.int32),
+            pltpu.SMEM(ids, jnp.int32),
+            pltpu.SMEM(tile_counts.shape, jnp.int32),
+            pltpu.VMEM((blocks, part_rows, length), bf16),
+            pltpu.VMEM((blocks, part_rows, length), bf16),
+            pltpu.VMEM((blocks, part_rows, length), bf16),
             pltpu.VMEM((kernels.shape[0] + 1, length, cells), bf16),
-            pltpu.VMEM((PER, cells // 128, rows, 128), jnp.float32),
-            pltpu.VMEM(stage, bf16),
-            pltpu.VMEM(stage, bf16),
-            pltpu.VMEM(stage, bf16),
-            pltpu.VMEM(half, bf16),
-            pltpu.VMEM(half, bf16),
-            pltpu.VMEM(stage, bf16),
-            pltpu.VMEM(stage, bf16),
-            pltpu.VMEM((STAGES, PER, 2, rows // 2, cells), bf16),
-            pltpu.SemaphoreType.DMA((9,)),
-            pltpu.SemaphoreType.DMA((2, STAGES)),
-            pltpu.SemaphoreType.DMA((2, STAGES)),
-            pltpu.SemaphoreType.DMA((2, STAGES)),
-            pltpu.SemaphoreType.DMA((2, STAGES)),
+            pltpu.VMEM((PER, cells // 128, rows, 128), f32),
+            pltpu.VMEM((STAGES, PER, rows, cells), f32),
+            pltpu.VMEM(stage, f32),
+            pltpu.VMEM(stage, f32),
+            pltpu.VMEM(stage, f32),
+            pltpu.VMEM(stage, bf16),
+            pltpu.VMEM(stage, bf16),
+            pltpu.VMEM(stage, bf16),
+            pltpu.VMEM(stage, bf16),
+            pltpu.VMEM(stage, bf16),
+            pltpu.VMEM(stage, bf16),
+            pltpu.VMEM((STAGES, PER, 2, part_rows, cells), bf16),
+            pltpu.SemaphoreType.DMA((6,)),
+            pltpu.SemaphoreType.DMA((7,)),
+            pltpu.SemaphoreType.DMA((7,)),
+            pltpu.SemaphoreType.DMA((3, STAGES)),
+            pltpu.SemaphoreType.DMA((3, STAGES)),
             pltpu.SemaphoreType.DMA((STAGES, 2)),
             pltpu.SemaphoreType.DMA((STAGES, 2)),
         ],
         compiler_params=pltpu.CompilerParams(
-            collective_id=0, has_side_effects=True, vmem_limit_bytes=44 << 20
+            collective_id=0, has_side_effects=True, vmem_limit_bytes=48 << 20
         ),
         name="grid_exchange",
-    )(
-        block_ids[0].T, kernel_ids[0].T, tile_counts,
-        visibilities.reshape(blocks, rows, length), kernels,
-    )
+    )(*(pltpu.with_memory_space_constraint(one, pltpu.HBM) for one in operands))
     nchan = n_chan * ch_dev
     tiles = wedge_mask.shape[0]
     vmem = pl.BlockSpec(memory_space=pltpu.VMEM)

time: 131 us -> 116 us (0.89)
  Pallas kernels: 126 us -> 116 us
  local copies, waits for them, and re-layouts: 4.27 us -> 0.01 us
    pallas_call x1, Pallas kernels: 119 us -> 110 us  [local(): pl.pallas_call(functools.partial(grid_kernel, n_chan, n_bl), out_shape=ja...]
    unnamed x12 -> x4, local copies, waits for them, and re-layouts: 4.27 us -> 0.01 us
where the time goes in v3:
time: 116 us
  Pallas kernels  116 us (100%)
    pallas_call x1, Pallas kernels, local(): pl.pallas_call(functools.partial(grid_kernel, n_chan, n_bl), out_shape=ja...  110 us
    pallas_call x1, Pallas kernels, local(): pl.pallas_call(delay_kernel, out_shape=jax.ShapeDtypeStruct(result, jnp.f...  6.56 us

profile of v3, /device:TPU:1, one launch (start us, length us, event | category | flops | bytes accessed | tf_op | source)
XLA Modules:
  0.0 116.2 jit_solution(4379468235929076190)
XLA Ops:
  0.0 0.0 copy-start
  0.0 0.0 copy-start.1
  0.0 109.6 %grid_exchange.1 = bf16[2,2,32,48,256]{4,3,2,1,0:T(8,128)(2,1)S(1)} custom-call(s32[8,256]{1,0:T(8,128)} %bitcast.10, s32[8,256]{1,0:T(8,128)} %bitcast.11, s32[1,256]{1,0:T(1,128)} %cnt_hbm.1, bf16[256,96,128]{2,1,0:T(8,128)(2,1)} %bitcast.9, bf16[64,128,256]{2,1,0:T(8,128)(2,1)} %ker_hbm.1), custom_call_target="tpu_custom_call" | custom-call | tf_op jit(solution)/shard_map/grid_exchange/pallas_call | solution.py:318
  109.6 0.0 copy-done
  109.6 0.0 copy-done.1
  109.6 6.6 %delay_transform.1 = f32[2,2,256,1536]{3,2,1,0:T(8,128)} custom-call(bf16[2,2,1536,256]{3,2,1,0:T(8,128)(2,1)S(1)} %bitcast.8, bf16[2,1536,1536]{2,1,0:T(8,128)(2,1)S(1)} %copy-done, s32[2,1536]{1,0:T(2,128)S(1)} %copy-done.1), custom_call_target="tpu_custom_call" | custom-call | flops 4831838208 | bytes 26214400 | tf_op jit(solution)/shard_map/delay_transform/pallas_call | solution.py:366
Async XLA Ops:
  0.0 109.6 %copy-start = (bf16[2,1536,1536]{2,1,0:T(8,128)(2,1)S(1)}, bf16[2,1536,1536]{2,1,0:T(8,128)(2,1)}, u32[]{:S(2)}) copy-start(bf16[2,1536,1536]{2,1,0:T(8,128)(2,1)} %constant.2.clone.table) | copy-start | bytes 28311556
  0.0 109.6 %copy-start.1 = (s32[2,1536]{1,0:T(2,128)S(1)}, s32[2,1536]{1,0:T(2,128)}, u32[]{:S(2)}) copy-start(s32[2,1536]{1,0:T(2,128)} %keep.1) | copy-start | bytes 36868

commit v4 on v3

--- a/solution.py
+++ b/solution.py
@@ -11,8 +11,15 @@
 from jax.sharding import PartitionSpec as P
 
 MESH = pl.DeviceIdType.MESH
-STAGES = 16
-PER = 4
+STAGES = 32
+OFFSETS = (
+    (0, 0), (0, 1), (3, 0), (0, 3), (1, 0), (1, 1), (3, 3), (0, 2),
+    (1, 3), (3, 1), (2, 0), (1, 2), (2, 3), (3, 2), (2, 1), (2, 2),
+)
+PER = 2
+LAG = 3
+OWN_LAG = 6
+SLICE_AT = STAGES // 2 + OWN_LAG + 1
 
 
 def tables(nchan, ch_dev):
@@ -32,11 +39,12 @@
 
 
 def grid_kernel(
-    n_chan, n_bl, bid_hbm, kid_hbm, cnt_hbm, vis_hbm, ker_hbm, grid_out,
+    n_chan, n_bl, bid_hbm, kid_hbm, cnt_hbm, vis_hbm, ker_hbm, table_hbm, keep_hbm, grid_out, out,
     bid, kid, cnt, bid_in, kid_in, cnt_in, bid_out, kid_out, cnt_out,
     vis_hub, vis_leaf, vis_in, ker, sums,
     sum_own, sum_inner, sum_far, sum_outer,
     to_inner, to_far, to_outer, from_inner, from_far, from_outer, own,
+    grid_first, left, table, keep,
     load_sem, vis_s, vis_r, nbr_s, nbr_r, own_s, own_r,
 ):
     chan = lax.axis_index("chan")
@@ -109,15 +117,35 @@
         copy.start()
     for one in loads:
         one.wait()
+    late = [
+        pltpu.make_async_copy(src, dst, load_sem.at[6 + q])
+        for q, (src, dst) in enumerate(((keep_hbm, keep), (table_hbm, table)))
+    ]
+    for one in late:
+        one.start()
+    for copy in vis_copies[:3]:
+        copy.wait_recv()
+    arrived = [
+        pltpu.make_async_copy(src, dst, load_sem.at[q])
+        for q, (src, dst) in enumerate(((bid_in, bid_out), (kid_in, kid_out), (cnt_in, cnt_out)))
+    ]
+    for one in arrived:
+        one.start()
+    for one in arrived:
+        one.wait()
+
+    half = STAGES // 2
 
     def owner(s, e):
-        m = STAGES - 1 - s
-        dz = lax.rem(m, 4)
-        dx = lax.rem(lax.div(m, 4) + m, 4)
+        m = half - 1 - lax.rem(s, half)
+        dz, dx = 0, 0
+        for at, (first_of, second_of) in enumerate(OFFSETS):
+            dz = jnp.where(m == at, first_of, dz)
+            dx = jnp.where(m == at, second_of, dx)
         return (lax.rem(row + dz, 4) * 4 + lax.rem(col + dx, 4)) * 2 + lax.rem(core + e, 2)
 
     def tile_of(s, j, plane):
-        return (owner(s, j // 2) * n_bl + plane) * 2 + j % 2
+        return (owner(s, j) * n_bl + plane) * 2 + lax.div(s, half)
 
     def partial(tile, ids, sources):
         block_of, kind_of, count_of = ids
@@ -140,24 +168,21 @@
 
     def first(s, carry):
         for j in range(PER):
-            sum_far[s, j] = partial(tile_of(s, j, far), mine, [vis_hub])
-            sum_inner[s, j] = partial(tile_of(s, j, inner), mine, [vis_hub])
-            sum_outer[s, j] = partial(tile_of(s, j, outer), mine, [vis_hub])
-            sum_own[s, j] = partial(tile_of(s, j, y), mine, [vis_hub, vis_leaf])
+            for plane, kept, sources in (
+                (far, sum_far, [vis_hub]),
+                (inner, sum_inner, [vis_hub]),
+                (outer, sum_outer, [vis_hub]),
+                (y, sum_own, [vis_hub, vis_leaf]),
+            ):
+                kept[s, j] = partial(tile_of(s, j, plane), mine, sources).astype(kept.dtype)
         return carry
 
     lax.fori_loop(0, STAGES, first, 0)
 
-    for copy in vis_copies:
+    for one in late:
+        one.wait()
+    for copy in vis_copies[3:]:
         copy.wait_recv()
-    arrived = [
-        pltpu.make_async_copy(src, dst, load_sem.at[q])
-        for q, (src, dst) in enumerate(((bid_in, bid_out), (kid_in, kid_out), (cnt_in, cnt_out)))
-    ]
-    for one in arrived:
-        one.start()
-    for one in arrived:
-        one.wait()
 
     def far_copy(s):
         return remote(to_far.at[s], from_far.at[s], nbr_s.at[0, s], nbr_r.at[0, s], inner)
@@ -168,18 +193,32 @@
     def outer_copy(s):
         return remote(to_outer.at[s], from_outer.at[s], nbr_s.at[2, s], nbr_r.at[2, s], outer)
 
-    def own_copy(s, e):
+    def own_copy(s, e, target):
         return pltpu.make_async_remote_copy(
-            src_ref=own.at[s, pl.ds(2 * e, 2)],
-            dst_ref=grid_out.at[:, :, chan],
+            src_ref=own.at[s, e], dst_ref=target.at[:, chan],
             send_sem=own_s.at[s, e], recv_sem=own_r.at[s, e],
             device_id=(owner(s, e), y), device_id_type=MESH,
         )
 
-    def self_copy():
-        return pltpu.make_async_copy(
-            own.at[STAGES - 1, pl.ds(0, 2)], grid_out.at[:, :, chan], own_r.at[STAGES - 1, 0]
-        )
+    def self_copy(s, target):
+        return pltpu.make_async_copy(own.at[s, 0], target.at[:, chan], own_r.at[s, 0])
+
+    def send_own(s, target, last):
+        @pl.when(s < last)
+        def _():
+            own_copy(s, 0, target).start()
+
+        own_copy(s, 1, target).start()
+
+        @pl.when(s == last)
+        def _():
+            self_copy(last, target).start()
+
+    nchan, width = left.shape[2], left.shape[1]
+    slices = nchan // 2 // width
+
+    def lanes_of(q):
+        return [pl.multiple_of(side * (nchan // 2) + q * width, width) for side in range(2)]
 
     def step(it, carry):
         @pl.when(it < STAGES)
@@ -187,37 +226,37 @@
             s = it
             for j in range(PER):
                 to_far[s, j] = (
-                    sum_far[s, j] + partial(tile_of(s, j, far), others, [vis_in])
+                    sum_far[s, j].astype(jnp.float32) + partial(tile_of(s, j, far), others, [vis_in])
                 ).astype(jnp.bfloat16)
             far_copy(s).start()
+
+        @pl.when((it >= LAG) & (it < STAGES + LAG))
+        def _():
+            s = it - LAG
             for j in range(PER):
                 to_inner[s, j] = (
-                    sum_inner[s, j] + partial(tile_of(s, j, inner), others, [vis_in])
+                    sum_inner[s, j].astype(jnp.float32) + partial(tile_of(s, j, inner), others, [vis_in])
                 ).astype(jnp.bfloat16)
             inner_copy(s).start()
-
-        @pl.when((it >= 1) & (it < STAGES + 1))
-        def _():
-            s = it - 1
             far_copy(s).wait_recv()
             for j in range(PER):
                 to_outer[s, j] = (
-                    sum_outer[s, j] + from_far[s, j].astype(jnp.float32)
+                    sum_outer[s, j].astype(jnp.float32) + from_far[s, j].astype(jnp.float32)
                 ).astype(jnp.bfloat16)
             outer_copy(s).start()
 
-        @pl.when(it >= 2)
-        def _():
-            s = it - 2
+        @pl.when(it >= OWN_LAG)
+        def _():
+            s = it - OWN_LAG
             inner_copy(s).wait_recv()
             outer_copy(s).wait_recv()
             for j in range(PER):
                 hub_rows = (
-                    sum_own[s, j, :part_rows]
+                    sum_own[s, j, :part_rows].astype(jnp.float32)
                     + partial(tile_of(s, j, y), others, [vis_in])
                     + from_inner[s, j].astype(jnp.float32)
                 )
-                leaf_rows = sum_own[s, j, part_rows:] + from_outer[s, j].astype(jnp.float32)
+                leaf_rows = sum_own[s, j, part_rows:].astype(jnp.float32) + from_outer[s, j].astype(jnp.float32)
                 for lane in range(sums.shape[1]):
                     at = slice(lane * 128, lane * 128 + 128)
                     sums[j, lane, pl.ds(hub_at, part_rows)] = hub_rows[:, at]
@@ -235,19 +274,48 @@
                     ]
                     own[s, j, odd] = jnp.concatenate(sorted_rows, axis=1).astype(jnp.bfloat16)
 
-            @pl.when(s < STAGES - 1)
+            @pl.when(s < half)
             def _():
-                own_copy(s, 0).start()
-
-            own_copy(s, 1).start()
-
-            @pl.when(s == STAGES - 1)
+                send_own(s, grid_first, half - 1)
+
+            @pl.when(s >= half)
             def _():
-                self_copy().start()
+                send_own(s, grid_out, STAGES - 1)
+
+        @pl.when(it == SLICE_AT)
+        def _():
+            def received(s, c):
+                @pl.when(s < half - 1)
+                def _():
+                    own_copy(s, 0, grid_first).wait_recv()
+
+                own_copy(s, 1, grid_first).wait_recv()
+                return c
+
+            lax.fori_loop(0, half, received, 0)
+            self_copy(half - 1, grid_first).wait()
+
+        @pl.when((it >= SLICE_AT) & (it < SLICE_AT + 2))
+        def _():
+            odd = it - SLICE_AT
+            left[odd] = grid_first[odd].reshape(nchan, width).T
+
+        @pl.when((it >= SLICE_AT + 2) & (it < SLICE_AT + 2 + 2 * slices))
+        def _():
+            c = it - SLICE_AT - 2
+            part, q = lax.div(c, slices), lax.rem(c, slices)
+            at = pl.multiple_of(part * (nchan // 2) + q * width, width)
+            values = delay_slice(
+                [left[odd] for odd in range(2)],
+                [table[odd, :, pl.ds(at, width)] for odd in range(2)],
+            )
+            for lane, value in zip(lanes_of(q), values):
+                bins = keep[0:1, pl.ds(lane, width)].astype(jnp.float32) * (1.0 / math.sqrt(nchan))
+                out[part, :, pl.ds(lane, width)] = value * bins
 
         return carry
 
-    lax.fori_loop(0, STAGES + 2, step, 0)
+    lax.fori_loop(0, STAGES + OWN_LAG, step, 0)
 
     for copy in vis_copies:
         copy.wait_send()
@@ -256,47 +324,65 @@
         for copy in (far_copy(s), inner_copy(s), outer_copy(s)):
             copy.wait_send()
 
-        @pl.when(s < STAGES - 1)
-        def _():
-            own_copy(s, 0).wait()
-
-        own_copy(s, 1).wait()
+        @pl.when(s < half)
+        def _():
+            @pl.when(s < half - 1)
+            def _():
+                own_copy(s, 0, grid_first).wait_send()
+
+            own_copy(s, 1, grid_first).wait_send()
+
+        @pl.when(s >= half)
+        def _():
+            @pl.when(s < STAGES - 1)
+            def _():
+                own_copy(s, 0, grid_out).wait()
+
+            own_copy(s, 1, grid_out).wait()
+
         return carry
 
     lax.fori_loop(0, STAGES, drain, 0)
-    self_copy().wait()
-
-
-def delay_kernel(grids, table, keep, out_hbm, left, out, sem):
-    tiles, parities, nchan, cells = grids.shape
+    self_copy(STAGES - 1, grid_out).wait()
+
+
+def delay_slice(left, right):
+    even_sum, odd_sum = (
+        jnp.dot(one, two, preferred_element_type=jnp.float32) for one, two in zip(left, right)
+    )
+    return even_sum + odd_sum, even_sum - odd_sum
+
+
+def delay_kernel(grids, table, keep, first_tile, out_hbm, left, out, sem, first_sem):
+    parities, nchan, cells = grids.shape
     half = nchan // 2
     width = cells
     scale = 1.0 / math.sqrt(nchan)
     copies = []
-    for t in range(tiles):
-        for odd in range(parities):
-            left[t, odd] = grids[t, odd].T
-        for part in range(2):
-            for q in range(half // width):
-                at = part * half + q * width
-                even_sum, odd_sum = (
-                    jnp.dot(
-                        left[t, odd], table[odd, :, at : at + width],
-                        preferred_element_type=jnp.float32,
-                    )
-                    for odd in range(2)
+    for part in range(2):
+        copy = pltpu.make_async_copy(first_tile.at[part], out_hbm.at[0, part], first_sem.at[part])
+        copy.start()
+        copies.append(copy)
+    for odd in range(parities):
+        left[odd] = grids[odd].T
+    for part in range(2):
+        for q in range(half // width):
+            at = part * half + q * width
+            values = delay_slice(
+                [left[odd] for odd in range(2)],
+                [table[odd, :, at : at + width] for odd in range(2)],
+            )
+            for side, value in enumerate(values):
+                lane = side * half + q * width
+                bins = keep[1:2, lane : lane + width].astype(jnp.float32) * scale
+                out[part, :, lane : lane + width] = value * bins
+                copy = pltpu.make_async_copy(
+                    out.at[part, :, pl.ds(lane, width)],
+                    out_hbm.at[1, part, :, pl.ds(lane, width)],
+                    sem.at[2 * (part * (half // width) + q) + side],
                 )
-                for side, value in enumerate((even_sum + odd_sum, even_sum - odd_sum)):
-                    lane = side * half + q * width
-                    bins = keep[t : t + 1, lane : lane + width].astype(jnp.float32) * scale
-                    out[t, part, :, lane : lane + width] = value * bins
-                    copy = pltpu.make_async_copy(
-                        out.at[t, part, :, pl.ds(lane, width)],
-                        out_hbm.at[t, part, :, pl.ds(lane, width)],
-                        sem.at[len(copies)],
-                    )
-                    copy.start()
-                    copies.append(copy)
+                copy.start()
+                copies.append(copy)
     for copy in copies:
         copy.wait()
 
@@ -313,13 +399,19 @@
     ids = (block_ids.shape[2], block_ids.shape[1])
     operands = (
         block_ids[0].T, kernel_ids[0].T, tile_counts,
-        visibilities.reshape(blocks, rows, length), kernels,
+        visibilities.reshape(blocks, rows, length), kernels, table, wedge_mask,
     )
-    grids = pl.pallas_call(
+    nchan = n_chan * ch_dev
+    tiles = wedge_mask.shape[0]
+    result = (tiles, 2, cells, nchan)
+    grids, first_tile = pl.pallas_call(
         functools.partial(grid_kernel, n_chan, n_bl),
-        out_shape=jax.ShapeDtypeStruct((2, 2, n_chan, part_rows, cells), bf16),
+        out_shape=(
+            jax.ShapeDtypeStruct((2, n_chan, part_rows, cells), bf16),
+            jax.ShapeDtypeStruct(result[1:], f32),
+        ),
         in_specs=[hbm] * len(operands),
-        out_specs=pl.BlockSpec(memory_space=pl.ANY),
+        out_specs=(pl.BlockSpec(memory_space=pl.ANY), pl.BlockSpec(memory_space=pltpu.VMEM)),
         scratch_shapes=[
             pltpu.SMEM(ids, jnp.int32),
             pltpu.SMEM(ids, jnp.int32),
@@ -335,10 +427,10 @@
             pltpu.VMEM((blocks, part_rows, length), bf16),
             pltpu.VMEM((kernels.shape[0] + 1, length, cells), bf16),
             pltpu.VMEM((PER, cells // 128, rows, 128), f32),
-            pltpu.VMEM((STAGES, PER, rows, cells), f32),
-            pltpu.VMEM(stage, f32),
-            pltpu.VMEM(stage, f32),
-            pltpu.VMEM(stage, f32),
+            pltpu.VMEM((STAGES, PER, rows, cells), bf16),
+            pltpu.VMEM(stage, bf16),
+            pltpu.VMEM(stage, bf16),
+            pltpu.VMEM(stage, bf16),
             pltpu.VMEM(stage, bf16),
             pltpu.VMEM(stage, bf16),
             pltpu.VMEM(stage, bf16),
@@ -346,7 +438,11 @@
             pltpu.VMEM(stage, bf16),
             pltpu.VMEM(stage, bf16),
             pltpu.VMEM((STAGES, PER, 2, part_rows, cells), bf16),
-            pltpu.SemaphoreType.DMA((6,)),
+            pltpu.VMEM((2, n_chan, part_rows, cells), bf16),
+            pltpu.VMEM((2, cells, nchan), bf16),
+            pltpu.VMEM(table.shape, bf16),
+            pltpu.VMEM(wedge_mask.shape, jnp.int32),
+            pltpu.SemaphoreType.DMA((8,)),
             pltpu.SemaphoreType.DMA((7,)),
             pltpu.SemaphoreType.DMA((7,)),
             pltpu.SemaphoreType.DMA((3, STAGES)),
@@ -355,30 +451,31 @@
             pltpu.SemaphoreType.DMA((STAGES, 2)),
         ],
         compiler_params=pltpu.CompilerParams(
-            collective_id=0, has_side_effects=True, vmem_limit_bytes=48 << 20
+            collective_id=0, has_side_effects=True, vmem_limit_bytes=47 << 20
         ),
         name="grid_exchange",
     )(*(pltpu.with_memory_space_constraint(one, pltpu.HBM) for one in operands))
-    nchan = n_chan * ch_dev
-    tiles = wedge_mask.shape[0]
     vmem = pl.BlockSpec(memory_space=pltpu.VMEM)
-    result = (tiles, 2, cells, nchan)
     return pl.pallas_call(
         delay_kernel,
-        out_shape=jax.ShapeDtypeStruct(result, jnp.float32),
-        in_specs=[vmem, vmem, vmem],
+        out_shape=jax.ShapeDtypeStruct(result, f32),
+        in_specs=[vmem, vmem, vmem, vmem],
         out_specs=hbm,
         scratch_shapes=[
-            pltpu.VMEM((tiles, 2, cells, nchan), bf16),
-            pltpu.VMEM(result, jnp.float32),
-            pltpu.SemaphoreType.DMA((4 * tiles * nchan // 2 // cells,)),
+            pltpu.VMEM((2, cells, nchan), bf16),
+            pltpu.VMEM(result[1:], f32),
+            pltpu.SemaphoreType.DMA((2 * nchan // cells,)),
+            pltpu.SemaphoreType.DMA((2,)),
         ],
-        compiler_params=pltpu.CompilerParams(vmem_limit_bytes=34 << 20),
+        compiler_params=pltpu.CompilerParams(vmem_limit_bytes=26 << 20),
         cost_estimate=pl.CostEstimate(
-            flops=tiles * 4 * cells * nchan * nchan, bytes_accessed=25 << 20, transcendentals=0
+            flops=4 * cells * nchan * nchan, bytes_accessed=16 << 20, transcendentals=0
         ),
         name="delay_transform",
-    )(grids.reshape(2, 2, nchan, cells), table, wedge_mask)
+    )(
+        grids.reshape(2, nchan, cells), table, wedge_mask,
+        first_tile,
+    )
 
 
 def solution(mesh):

time: 116 us -> 111 us (0.957)
  Pallas kernels: 116 us -> 110 us
    pallas_call x2, Pallas kernels: 116 us -> 110 us  [the longest x1 107 us: local(): pl.pallas_call(functools.partial(grid_kernel, n_chan, n_bl), out_shape=(j...]
where the time goes in v4:
time: 111 us
  Pallas kernels  110 us (99%)
    pallas_call x1, Pallas kernels, local(): pl.pallas_call(functools.partial(grid_kernel, n_chan, n_bl), out_shape=(j...  107 us
    pallas_call x1, Pallas kernels, local(): pl.pallas_call(delay_kernel, out_shape=jax.ShapeDtypeStruct(result, f32),...  3.78 us

profile of v4, /device:TPU:1, one launch (start us, length us, event | category | flops | bytes accessed | tf_op | source)
XLA Modules:
  0.0 110.5 jit_solution(8485044746342288082)
XLA Ops:
  0.0 0.0 slice-start
  0.0 0.0 slice-start.1
  0.0 0.0 slice-start.2
  0.0 0.0 copy-start
  0.0 106.7 %grid_exchange.1 = (bf16[2,32,48,256]{3,2,1,0:T(8,128)(2,1)S(1)}, f32[2,256,1536]{2,1,0:T(8,128)S(1)}) custom-call(s32[8,256]{1,0:T(8,128)} %bitcast.12, s32[8,256]{1,0:T(8,128)} %bitcast.13, s32[1,256]{1,0:T(1,128)} %cnt_hbm.1, bf16[256,96,128]{2,1,0:T(8,128)(2,1)} %bitcast.11, bf16[64,128,256]{2,1,0:T(8,128)(2,1)} %ker_hbm.1, ...), custom_call_target="tpu_custom_call" | custom-call | tf_op jit(solution)/shard_map/grid_exchange/pallas_call | solution.py:407
  106.7 0.0 slice-done
  106.7 0.0 slice-done.1
  106.7 0.0 slice-done.2
  106.8 0.0 copy-done
  106.8 3.8 %delay_transform.1 = f32[2,2,256,1536]{3,2,1,0:T(8,128)} custom-call(bf16[2,1536,256]{2,1,0:T(8,128)(2,1)S(1)} %bitcast.10, bf16[2,1536,1536]{2,1,0:T(8,128)(2,1)S(1)} %bitcast.9, s32[2,1536]{1,0:T(2,128)S(1)} %copy-done, f32[2,256,1536]{2,1,0:T(8,128)S(1)} %get-tuple-element.8.first_tile), custom_call_target="tpu_custom_call" | custom-call | flops 2415919104 | bytes 16777216 | tf_op jit(solution)/shard_map/delay_transform/pallas_call | solution.py:459
  (1 shorter events, 0.0 us)
Async XLA Ops:
  0.0 106.7 %slice-start = ((s8[9437184]{0:T(1024)(128)(4,1)}), s8[4194304]{0:T(1024)(128)(4,1)S(1)}, s32[]{:S(2)}) async-start(s8[9437184]{0:T(1024)(128)(4,1)} %bitcast.8), calls=%async_computation | async-start | bytes 8388608
  0.0 106.7 %slice-start.1 = ((s8[9437184]{0:T(1024)(128)(4,1)}), s8[4194304]{0:T(1024)(128)(4,1)S(1)}, s32[]{:S(2)}) async-start(s8[9437184]{0:T(1024)(128)(4,1)} %bitcast.8), calls=%async_computation.1 | async-start | bytes 8388608
  0.0 106.7 %slice-start.2 = ((s8[9437184]{0:T(1024)(128)(4,1)}), s8[1048576]{0:T(1024)(128)(4,1)S(1)}, s32[]{:S(2)}) async-start(s8[9437184]{0:T(1024)(128)(4,1)} %bitcast.8), calls=%async_computation.2 | async-start | bytes 2097152
  0.0 106.7 %copy-start = (s32[2,1536]{1,0:T(2,128)S(1)}, s32[2,1536]{1,0:T(2,128)}, u32[]{:S(2)}) copy-start(s32[2,1536]{1,0:T(2,128)} %keep.1) | copy-start | bytes 36868

commit v5 on v4

--- a/solution.py
+++ b/solution.py
@@ -18,8 +18,8 @@
 )
 PER = 2
 LAG = 3
-OWN_LAG = 6
-SLICE_AT = STAGES // 2 + OWN_LAG + 1
+OWN_LAG = 7
+SLICE_AT = STAGES // 2 + OWN_LAG + 2
 
 
 def tables(nchan, ch_dev):
@@ -66,6 +66,17 @@
     leaf_at = pl.multiple_of((1 - hub) * part_rows, part_rows)
     cut = blocks // 4
 
+    barrier = pltpu.get_barrier_semaphore()
+
+    def greet(o, carry):
+        pl.semaphore_signal(
+            barrier, inc=1, device_id=(lax.rem(chan + o, n_chan), y), device_id_type=MESH
+        )
+        return carry
+
+    for other in (outer, inner):
+        pl.semaphore_signal(barrier, inc=1, device_id=(chan, other), device_id_type=MESH)
+    lax.fori_loop(1, n_chan, greet, 0, unroll=True)
     loads = [
         pltpu.make_async_copy(src, dst, load_sem.at[q])
         for q, (src, dst) in enumerate(
@@ -81,17 +92,6 @@
         one.start()
     ker[kinds] = jnp.zeros(ker.shape[1:], ker.dtype)
 
-    barrier = pltpu.get_barrier_semaphore()
-
-    def greet(o, carry):
-        pl.semaphore_signal(
-            barrier, inc=1, device_id=(lax.rem(chan + o, n_chan), y), device_id_type=MESH
-        )
-        return carry
-
-    for other in (outer, inner):
-        pl.semaphore_signal(barrier, inc=1, device_id=(chan, other), device_id_type=MESH)
-    lax.fori_loop(1, n_chan, greet, 0)
     pl.semaphore_wait(barrier, n_chan + 1)
 
     def remote(src, dst, send, recv, plane):
@@ -248,14 +248,15 @@
         @pl.when(it >= OWN_LAG)
         def _():
             s = it - OWN_LAG
+            gridded = [
+                sum_own[s, j, :part_rows].astype(jnp.float32)
+                + partial(tile_of(s, j, y), others, [vis_in])
+                for j in range(PER)
+            ]
             inner_copy(s).wait_recv()
             outer_copy(s).wait_recv()
             for j in range(PER):
-                hub_rows = (
-                    sum_own[s, j, :part_rows].astype(jnp.float32)
-                    + partial(tile_of(s, j, y), others, [vis_in])
-                    + from_inner[s, j].astype(jnp.float32)
-                )
+                hub_rows = gridded[j] + from_inner[s, j].astype(jnp.float32)
                 leaf_rows = sum_own[s, j, part_rows:].astype(jnp.float32) + from_outer[s, j].astype(jnp.float32)
                 for lane in range(sums.shape[1]):
                     at = slice(lane * 128, lane * 128 + 128)
@@ -363,15 +364,11 @@
         copy = pltpu.make_async_copy(first_tile.at[part], out_hbm.at[0, part], first_sem.at[part])
         copy.start()
         copies.append(copy)
-    for odd in range(parities):
-        left[odd] = grids[odd].T
+    turned = [grids[odd].T for odd in range(parities)]
     for part in range(2):
         for q in range(half // width):
             at = part * half + q * width
-            values = delay_slice(
-                [left[odd] for odd in range(2)],
-                [table[odd, :, at : at + width] for odd in range(2)],
-            )
+            values = delay_slice(turned, [table[odd, :, at : at + width] for odd in range(2)])
             for side, value in enumerate(values):
                 lane = side * half + q * width
                 bins = keep[1:2, lane : lane + width].astype(jnp.float32) * scale

time: 111 us -> 110 us (level)
  no operation moved by 1% of the time
where the time goes in v5:
time: 110 us
  Pallas kernels  110 us (100%)
    pallas_call x1, Pallas kernels, local(): pl.pallas_call(functools.partial(grid_kernel, n_chan, n_bl), out_shape=(j...  106 us
    pallas_call x1, Pallas kernels, local(): pl.pallas_call(delay_kernel, out_shape=jax.ShapeDtypeStruct(result, f32),...  3.78 us

profile of v5, /device:TPU:1, one launch (start us, length us, event | category | flops | bytes accessed | tf_op | source)
XLA Modules:
  0.0 109.6 jit_solution(10402863664708343318)
XLA Ops:
  0.0 0.0 slice-start
  0.0 0.0 slice-start.1
  0.0 0.0 slice-start.2
  0.0 0.0 copy-start
  0.0 105.7 %grid_exchange.1 = (bf16[2,32,48,256]{3,2,1,0:T(8,128)(2,1)S(1)}, f32[2,256,1536]{2,1,0:T(8,128)S(1)}) custom-call(s32[8,256]{1,0:T(8,128)} %bitcast.12, s32[8,256]{1,0:T(8,128)} %bitcast.13, s32[1,256]{1,0:T(1,128)} %cnt_hbm.1, bf16[256,96,128]{2,1,0:T(8,128)(2,1)} %bitcast.11, bf16[64,128,256]{2,1,0:T(8,128)(2,1)} %ker_hbm.1, ...), custom_call_target="tpu_custom_call" | custom-call | tf_op jit(solution)/shard_map/grid_exchange/pallas_call | solution.py:404
  105.8 0.0 slice-done
  105.8 0.0 slice-done.1
  105.8 0.0 slice-done.2
  105.8 0.0 copy-done
  105.8 3.8 %delay_transform.1 = f32[2,2,256,1536]{3,2,1,0:T(8,128)} custom-call(bf16[2,1536,256]{2,1,0:T(8,128)(2,1)S(1)} %bitcast.10, bf16[2,1536,1536]{2,1,0:T(8,128)(2,1)S(1)} %bitcast.9, s32[2,1536]{1,0:T(2,128)S(1)} %copy-done, f32[2,256,1536]{2,1,0:T(8,128)S(1)} %get-tuple-element.8.first_tile), custom_call_target="tpu_custom_call" | custom-call | flops 2415919104 | bytes 16777216 | tf_op jit(solution)/shard_map/delay_transform/pallas_call | solution.py:456
  (1 shorter events, 0.0 us)
Async XLA Ops:
  0.0 105.8 %slice-start = ((s8[9437184]{0:T(1024)(128)(4,1)}), s8[4194304]{0:T(1024)(128)(4,1)S(1)}, s32[]{:S(2)}) async-start(s8[9437184]{0:T(1024)(128)(4,1)} %bitcast.8), calls=%async_computation | async-start | bytes 8388608
  0.0 105.8 %slice-start.1 = ((s8[9437184]{0:T(1024)(128)(4,1)}), s8[4194304]{0:T(1024)(128)(4,1)S(1)}, s32[]{:S(2)}) async-start(s8[9437184]{0:T(1024)(128)(4,1)} %bitcast.8), calls=%async_computation.1 | async-start | bytes 8388608
  0.0 105.8 %slice-start.2 = ((s8[9437184]{0:T(1024)(128)(4,1)}), s8[1048576]{0:T(1024)(128)(4,1)S(1)}, s32[]{:S(2)}) async-start(s8[9437184]{0:T(1024)(128)(4,1)} %bitcast.8), calls=%async_computation.2 | async-start | bytes 2097152
  0.0 105.8 %copy-start = (s32[2,1536]{1,0:T(2,128)S(1)}, s32[2,1536]{1,0:T(2,128)}, u32[]{:S(2)}) copy-start(s32[2,1536]{1,0:T(2,128)} %keep.1) | copy-start | bytes 36868

commit v6 on v5

--- a/solution.py
+++ b/solution.py
@@ -13,8 +13,8 @@
 MESH = pl.DeviceIdType.MESH
 STAGES = 32
 OFFSETS = (
-    (0, 0), (0, 1), (3, 0), (0, 3), (1, 0), (1, 1), (3, 3), (0, 2),
-    (1, 3), (3, 1), (2, 0), (1, 2), (2, 3), (3, 2), (2, 1), (2, 2),
+    (0, 0), (0, 1), (3, 0), (0, 3), (1, 0), (0, 2), (2, 0), (1, 1),
+    (3, 3), (1, 3), (3, 1), (2, 1), (1, 2), (2, 3), (3, 2), (2, 2),
 )
 PER = 2
 LAG = 3
@@ -208,8 +208,6 @@
         def _():
             own_copy(s, 0, target).start()
 
-        own_copy(s, 1, target).start()
-
         @pl.when(s == last)
         def _():
             self_copy(last, target).start()
@@ -255,7 +253,7 @@
             ]
             inner_copy(s).wait_recv()
             outer_copy(s).wait_recv()
-            for j in range(PER):
+            for j in reversed(range(PER)):
                 hub_rows = gridded[j] + from_inner[s, j].astype(jnp.float32)
                 leaf_rows = sum_own[s, j, part_rows:].astype(jnp.float32) + from_outer[s, j].astype(jnp.float32)
                 for lane in range(sums.shape[1]):
@@ -274,6 +272,15 @@
                         for lane in range(sums.shape[1])
                     ]
                     own[s, j, odd] = jnp.concatenate(sorted_rows, axis=1).astype(jnp.bfloat16)
+
+                if j:
+                    @pl.when(s < half)
+                    def _():
+                        own_copy(s, 1, grid_first).start()
+
+                    @pl.when(s >= half)
+                    def _():
+                        own_copy(s, 1, grid_out).start()
 
             @pl.when(s < half)
             def _():

time: 110 us -> 109 us (level)
  no operation moved by 1% of the time
where the time goes in v6:
time: 109 us
  Pallas kernels  109 us (100%)
    pallas_call x1, Pallas kernels, local(): pl.pallas_call(functools.partial(grid_kernel, n_chan, n_bl), out_shape=(j...  105 us
    pallas_call x1, Pallas kernels, local(): pl.pallas_call(delay_kernel, out_shape=jax.ShapeDtypeStruct(result, f32),...  3.77 us

profile of v6, /device:TPU:1, one launch (start us, length us, event | category | flops | bytes accessed | tf_op | source)
XLA Modules:
  0.0 109.2 jit_solution(14091589049513279181)
XLA Ops:
  0.0 0.0 slice-start
  0.0 0.0 slice-start.1
  0.0 0.0 slice-start.2
  0.0 0.0 copy-start
  0.0 105.4 %grid_exchange.1 = (bf16[2,32,48,256]{3,2,1,0:T(8,128)(2,1)S(1)}, f32[2,256,1536]{2,1,0:T(8,128)S(1)}) custom-call(s32[8,256]{1,0:T(8,128)} %bitcast.12, s32[8,256]{1,0:T(8,128)} %bitcast.13, s32[1,256]{1,0:T(1,128)} %cnt_hbm.1, bf16[256,96,128]{2,1,0:T(8,128)(2,1)} %bitcast.11, bf16[64,128,256]{2,1,0:T(8,128)(2,1)} %ker_hbm.1, ...), custom_call_target="tpu_custom_call" | custom-call | tf_op jit(solution)/shard_map/grid_exchange/pallas_call | solution.py:411
  105.4 0.0 slice-done
  105.4 0.0 slice-done.1
  105.4 0.0 slice-done.2
  105.4 0.0 copy-done
  105.4 3.8 %delay_transform.1 = f32[2,2,256,1536]{3,2,1,0:T(8,128)} custom-call(bf16[2,1536,256]{2,1,0:T(8,128)(2,1)S(1)} %bitcast.10, bf16[2,1536,1536]{2,1,0:T(8,128)(2,1)S(1)} %bitcast.9, s32[2,1536]{1,0:T(2,128)S(1)} %copy-done, f32[2,256,1536]{2,1,0:T(8,128)S(1)} %get-tuple-element.8.first_tile), custom_call_target="tpu_custom_call" | custom-call | flops 2415919104 | bytes 16777216 | tf_op jit(solution)/shard_map/delay_transform/pallas_call | solution.py:463
  (1 shorter events, 0.0 us)
Async XLA Ops:
  0.0 105.4 %slice-start = ((s8[9437184]{0:T(1024)(128)(4,1)}), s8[4194304]{0:T(1024)(128)(4,1)S(1)}, s32[]{:S(2)}) async-start(s8[9437184]{0:T(1024)(128)(4,1)} %bitcast.8), calls=%async_computation | async-start | bytes 8388608
  0.0 105.4 %slice-start.1 = ((s8[9437184]{0:T(1024)(128)(4,1)}), s8[4194304]{0:T(1024)(128)(4,1)S(1)}, s32[]{:S(2)}) async-start(s8[9437184]{0:T(1024)(128)(4,1)} %bitcast.8), calls=%async_computation.1 | async-start | bytes 8388608
  0.0 105.4 %slice-start.2 = ((s8[9437184]{0:T(1024)(128)(4,1)}), s8[1048576]{0:T(1024)(128)(4,1)S(1)}, s32[]{:S(2)}) async-start(s8[9437184]{0:T(1024)(128)(4,1)} %bitcast.8), calls=%async_computation.2 | async-start | bytes 2097152
  0.0 105.4 %copy-start = (s32[2,1536]{1,0:T(2,128)S(1)}, s32[2,1536]{1,0:T(2,128)}, u32[]{:S(2)}) copy-start(s32[2,1536]{1,0:T(2,128)} %keep.1) | copy-start | bytes 36868
